TPU v7x, 128 devices: a whole 4x4x4 slice. The times are simulated.
128 devices in a mesh: ping: 32 (over y, x, core), rng: 4 (over z).
Axes of the slice: x: 4, y: 4, z: 4, core: 2. Of those that a mesh axis runs over, the one named last changes fastest.
Arguments:
- echoes: bfloat16 [512, 2, 32, 8192], P('ping', None, None, 'rng'), may hold values from -36 to 36, as said below
- pairing: int32 [512, 2, 8], P('ping'), may hold values from 0 to 31, as said below
- footprint: int32 [32, 48], replicated, may hold values from 0 to 511, as said below
- counts: int32 [32], replicated, may hold values from 1 to 48, 512 in all
- offsets: int32 [32, 48], replicated, may hold values from -64 to 64
- earlier: bfloat16 [32, 2, 1024, 8192], P('ping', None, None, 'rng'), may hold values from -6 to 6
Outputs:
- image: bfloat16 [32, 2, 1024, 8192], P('ping', None, None, 'rng')
Inputs may be any that keep to these rules, and one draw needn't show every extreme that they name: `echoes`: the samples of a ping's pairing[p, 1] channels are partly a turned copy of ping p - 1's pairing[p, 0] channels. `pairing`: for each ping the 16 channels of its two rows are all different. `footprint`: the first counts[t] entries of row t are the pings that see tile t; the 48 entries of a row are different pings, and no aligned block of 16 pings (the pings of one ping owner, starting at a multiple of 16) holds more than 2 of them. `counts`: they sum to 512.
All inputs are finite; a program needn't handle non-finite values.
Results may differ from a plain program's by a relative error of at most 0.0053.
Values may be sent and summed in bfloat16 or wider, within the bound.
A program may use at most 192 MiB of HBM per device.

v0:
```python
import math

import jax
import jax.numpy as jnp
from jax import lax
from jax.sharding import PartitionSpec as P

C = 32
X = 1024
BAND = 64
MOST = 48
TILE_DEV = 1
PING_DEV = 16


phase_modulus = 4099
small_value = 1e-06


def passed_along(shard, axis, by):
    length = lax.axis_size(axis)
    pairs = [(i, i + by) for i in range(length) if 0 <= i + by < length]
    return lax.ppermute(shard, axis, pairs)


def prefix(shard, axis, combine, identity):
    length, position = (lax.axis_size(axis), lax.axis_index(axis))
    everything = lax.all_gather(shard, axis)
    start = jnp.broadcast_to(jnp.asarray(identity, shard.dtype), shard.shape)

    def step(k, before):
        reached = k < position
        new = combine(before, everything[k])
        return jnp.where(reached, new, before)

    return lax.fori_loop(0, length, step, start)


def with_halo(cells, sides, width):
    for axis, dim in sides:
        count = lax.axis_size(axis)
        ends = count - 1
        head = lax.slice_in_dim(cells, 0, width, axis=dim)
        tail = lax.slice_in_dim(cells, cells.shape[dim] - width, cells.shape[dim], axis=dim)
        cells = jnp.concatenate(
            [
                lax.ppermute(tail, axis, [(i, (i + 1) % count) for i in range(ends)]),
                cells,
                lax.ppermute(head, axis, [((i + 1) % count, i) for i in range(ends)]),
            ],
            axis=dim,
        )
    return cells


def weight_matrix(tile_id, ping_ids, shift_ids, live_rows, tile_count):
    spacing = TILE_DEV * X // PING_DEV
    column = jnp.arange(ping_ids.shape[0] * 2 * C, dtype=jnp.int32)
    part_of = column // C % 2
    channel = column % C
    ping_cols = jnp.repeat(ping_ids, 2 * C)
    shift_cols = jnp.repeat(shift_ids, 2 * C)
    live_cols = jnp.repeat(live_rows, 2 * C)
    pixels = jnp.arange(X, dtype=jnp.int32)
    offset = tile_id * X - ping_cols * spacing - 2 * channel
    folded = jnp.remainder(pixels[:, None] + offset[None, :], phase_modulus)
    square = jnp.remainder(folded * folded, phase_modulus)
    phases = square.astype(jnp.float32) * (2.0 * math.pi / phase_modulus) + shift_cols.astype(
        jnp.float32
    )[None, :] * (math.pi / 4.0)
    scales = live_cols / jnp.sqrt(jnp.float32(C) * tile_count.astype(jnp.float32))
    cosine = jnp.cos(phases) * scales[None, :]
    sines = jnp.sin(phases) * scales[None, :]
    upper_rows = jnp.where(part_of[None, :] == 0, cosine, -sines)
    lower_rows = jnp.where(part_of[None, :] == 0, sines, cosine)
    return jnp.concatenate([upper_rows, lower_rows], axis=0).astype(jnp.bfloat16)


def focus_tile(received_data, received_labels):
    flat_rows = received_data.reshape((-1,) + received_data.shape[2:])
    flat_labels = received_labels.reshape(-1, 4)
    live_int = (flat_labels[:, 0] >= 0).astype(jnp.int32)
    ping_ids = flat_labels[:, 1]
    shift_ids = flat_labels[:, 2]
    tile_id = flat_labels[0, 3]
    tile_count = jnp.sum(live_int)
    block_len = flat_rows.shape[3]
    weights = weight_matrix(tile_id, ping_ids, shift_ids, live_int.astype(jnp.float32), tile_count)
    product = jnp.dot(weights, flat_rows.reshape(-1, block_len), preferred_element_type=jnp.float32)
    return product.reshape(2, X, block_len)


def focus(received):
    received_data, received_labels = received
    results = [focus_tile(received_data[:, 0], received_labels[:, 0])]
    return jnp.stack(results, axis=0)


def per_device(echoes, pairing, footprint, counts, offsets, earlier):
    ping_dev = echoes.shape[0]
    owners = lax.axis_size("ping")
    own_index = lax.axis_index("ping")
    channel_ids = jnp.arange(C, dtype=jnp.int32)
    front_pick = (pairing[:, 0, :, None] == channel_ids).astype(jnp.bfloat16)
    rear_pick = (pairing[:, 1, :, None] == channel_ids).astype(jnp.bfloat16)
    rear_rows = jnp.einsum("pkc,pzcr->pzkr", rear_pick, echoes, preferred_element_type=jnp.float32)
    inner_rows = jnp.einsum(
        "pkc,pzcr->pzkr", front_pick[1:], echoes[:-1], preferred_element_type=jnp.float32
    )
    last_ping = passed_along(echoes[-1], "ping", 1)
    lead_rows = jnp.einsum(
        "kc,zcr->zkr", front_pick[0], last_ping, preferred_element_type=jnp.float32
    )
    front_rows = jnp.concatenate([lead_rows[None], inner_rows], axis=0)
    cross_sum = jnp.sum(
        front_rows[:, 0] * rear_rows[:, 1] - front_rows[:, 1] * rear_rows[:, 0], axis=(1, 2)
    )
    front_energy = jnp.sum(front_rows * front_rows, axis=(1, 2, 3))
    rear_energy = jnp.sum(rear_rows * rear_rows, axis=(1, 2, 3))
    cross_sum, front_energy, rear_energy = lax.psum((cross_sum, front_energy, rear_energy), "rng")
    increment = cross_sum / (jnp.sqrt(front_energy * rear_energy) + small_value)
    running = jnp.cumsum(increment)
    before_turn = prefix(running[-1], "ping", jnp.add, jnp.float32(0.0))
    track_turn = before_turn + running
    cosine = jnp.cos(track_turn)[:, None, None]
    sines = jnp.sin(track_turn)[:, None, None]
    real_part = echoes[:, 0].astype(jnp.float32)
    imag_part = echoes[:, 1].astype(jnp.float32)
    corrected = jnp.stack(
        [real_part * cosine + imag_part * sines, imag_part * cosine - real_part * sines], axis=1
    ).astype(jnp.bfloat16)
    tile_total = footprint.shape[0]
    slot_cap = -(-MOST // owners)
    positions = jnp.arange(MOST, dtype=jnp.int32)
    in_list = positions[None, :] < counts[:, None]
    from_here = in_list & (footprint // ping_dev == own_index)
    order_here = jnp.cumsum(from_here.astype(jnp.int32), axis=1) - 1
    slot_ids = jnp.arange(slot_cap, dtype=jnp.int32)
    select = (from_here[:, None, :] & (order_here[:, None, :] == slot_ids[None, :, None])).astype(
        jnp.int32
    )
    place_ids = jnp.sum(select * (positions + 1)[None, None, :], axis=2) - 1
    local_ids = jnp.sum(select * (footprint % ping_dev)[:, None, :], axis=2)
    ping_ids = jnp.sum(select * footprint[:, None, :], axis=2)
    shift_ids = jnp.sum(select * offsets[:, None, :], axis=2)
    tile_ids = jnp.broadcast_to(jnp.arange(tile_total, dtype=jnp.int32)[:, None], place_ids.shape)
    labels = jnp.stack([place_ids, ping_ids, shift_ids, tile_ids], axis=2).reshape(
        owners, tile_total // owners, slot_cap, 4
    )
    block_len = corrected.shape[3]
    source = with_halo(corrected, (("rng", 3),), BAND)

    def cut_window(local_one, offset_one):
        return lax.dynamic_slice(
            source, (local_one, 0, 0, BAND + offset_one), (1, 2, C, block_len)
        )[0]

    outgoing = jax.vmap(cut_window)(local_ids.reshape(-1), shift_ids.reshape(-1))
    outgoing = outgoing.reshape((owners, tile_total // owners, slot_cap, 2, C, block_len))
    contribution = focus(
        (
            lax.all_to_all(outgoing, "ping", split_axis=0, concat_axis=0, tiled=True),
            lax.all_to_all(labels, "ping", split_axis=0, concat_axis=0, tiled=True),
        )
    )
    return (earlier.astype(jnp.float32) + contribution).astype(jnp.bfloat16)


def solution(mesh):
    return jax.shard_map(
        per_device,
        mesh=mesh,
        in_specs=(
            P("ping", None, None, "rng"),
            P("ping", None, None),
            P(),
            P(),
            P(),
            P("ping", None, None, "rng"),
        ),
        out_specs=P("ping", None, None, "rng"),
        check_vma=False,
    )
```

profile of v0, /device:TPU:0, one launch (start us, length us, event | category | flops | bytes accessed | tf_op | source)
XLA Modules:
  0.0 670.0 jit_solution(12965153533234853385)
XLA Ops:
  5.7 9.0 %all-to-all-start = ((s32[32,1,2,4]{3,2,1,0:T(2,128)}), s32[32,1,2,4]{3,2,1,0:T(2,128)S(1)}, u32[]{:S(2)}, u32[]{:S(2)}) async-start(s32[32,1,2,4]{3,2,1,0:T(2,128)} %copy.64), calls=%async_computation | async-start | bytes 65536 | tf_op jit(solution)/shard_map/all_to_all | solution.py:163
  18.4 4.2 multiply_reduce_fusion
  26.4 11.8 %all-reduce.1 = (f32[16]{0:T(128)S(1)}, f32[16]{0:T(128)S(1)}, f32[16]{0:T(128)S(1)}) all-reduce(f32[16]{0:T(128)S(1)} %fusion.26, f32[16]{0:T(128)S(1)} %fusion.22, f32[16]{0:T(128)S(1)} %get-tuple-element.135), channel_id=1, replica_groups=mesh['ping'=32,'rng'=4] {'rng'}, use_global_device_ids=true, to_apply=%region_6.0 | all-reduce | flops 48 | bytes 384 | tf_op jit(solution)/shard_map/psum | solution.py:120
  40.1 65.6 %all-reduce = f32[32]{0:T(128)S(1)} all-reduce(f32[32]{0:T(128)S(1)} %bitcast_dynamic-update-slice_fusion.1), channel_id=2, replica_groups=mesh['ping'=32,'rng'=4] {'ping'}, use_global_device_ids=true, to_apply=%add | all-reduce | flops 32 | bytes 256 | tf_op jit(solution)/shard_map/all_gather | solution.py:28
  105.7 40.2 %while.14 = (s32[]{:T(128)}, f32[]{:T(128)}, s32[]{:T(128)}, f32[32]{0:T(128)S(1)}, s32[]{:T(128)}) while((s32[]{:T(128)}, f32[]{:T(128)}, s32[]{:T(128)}, f32[32]{0:T(128)S(1)}, s32[]{:T(128)}) %tuple.56), condition=%wide.region_13.14_spmd, body=%wide.region_12.13_spmd.sunk | while | flops 5 | bytes 107 | solution.py:36
  146.1 3.8 fusion.15
  155.2 4.4 collective-permute-done.2
  159.6 9.0 %concatenate.18 = bf16[16,2,32,2176]{3,2,1,0:T(8,128)(2,1)} concatenate(bf16[16,2,32,64]{3,2,1,0:T(8,128)(2,1)S(1)} %collective-permute-done.1, bf16[16,2,32,2048]{3,2,1,0:T(8,128)(2,1)} %pad_maximum_fusion.1, bf16[16,2,32,64]{3,2,1,0:T(8,128)(2,1)S(1)} %collective-permute-done.2), dimensions={3} | concatenate | bytes 8912896 | tf_op jit(solution)/shard_map/concatenate | solution.py:45
  168.7 238.2 %while.15 = (s32[]{:T(128)}, bf16[16,2,32,2176]{3,2,1,0:T(8,128)(2,1)}, s32[64,4]{0,1:T(4,128)S(1)}, bf16[64,1,2,32,2048]{4,3,2,1,0:T(8,128)(2,1)}, s32[]{:T(128)}) while((s32[]{:T(128)}, bf16[16,2,32,2176]{3,2,1,0:T(8,128)(2,1)}, s32[64,4]{0,1:T(4,128)S(1)}, bf16[64,1,2,32,2048]{4,3,2,1,0:T(8,128)(2,1)}, s32[]{:T(128)}) %tuple.59), condition=%wide.while_cond, body=%wide.while_body.sunk | while | flops 2 | bytes 525937 | solution.py:154
  184.2 3.1 bitcast_dynamic-update-slice_fusion.3
  199.1 3.1 bitcast_dynamic-update-slice_fusion.3
  214.0 3.1 bitcast_dynamic-update-slice_fusion.3
  240.0 3.1 bitcast_dynamic-update-slice_fusion.3
  247.5 3.1 bitcast_dynamic-update-slice_fusion.3
  295.9 3.1 bitcast_dynamic-update-slice_fusion.3
  299.6 3.1 bitcast_dynamic-update-slice_fusion.3
  307.1 3.1 bitcast_dynamic-update-slice_fusion.3
  318.3 3.1 bitcast_dynamic-update-slice_fusion.3
  355.5 3.1 bitcast_dynamic-update-slice_fusion.3
  406.9 5.3 all-to-all-start.1
  415.7 81.5 %select_convert_fusion.1 = (bf16[1024,4096]{1,0:T(8,128)(2,1)S(1)}, bf16[1024,4096]{1,0:T(8,128)(2,1)S(1)}) fusion(f32[4096]{0:T(1024)S(1)} %div.51, f32[4096]{0:T(1024)S(1)} %mul.166, s32[4096]{0:T(1024)S(1)} %fusion.51, pred[4096]{0:T(1024)(128)(4,1)S(1)} %fusion.48), kind=kLoop, calls=%fused_computation.13 | loop fusion | flops 100663296 | bytes 16830464 | tf_op jit(solution)/shard_map/convert.2
  497.2 7.1 %pad_maximum_fusion = bf16[2048,4096]{1,0:T(8,128)(2,1)} fusion(bf16[1024,4096]{1,0:T(8,128)(2,1)S(1)} %get-tuple-element.129, bf16[1024,4096]{1,0:T(8,128)(2,1)S(1)} %get-tuple-element.128), kind=kLoop, calls=%fused_computation.9 | loop fusion | flops 33554432 | bytes 33554432 | tf_op jit(solution)/shard_map/concatenate | solution.py:76
  504.4 121.0 %all-to-all-done.1 = bf16[32,1,2,2,32,2048]{5,4,3,2,1,0:T(8,128)(2,1)} async-done(((bf16[32,1,2,2,32,2048]{5,4,3,2,1,0:T(8,128)(2,1)}), bf16[32,1,2,2,32,2048]{5,4,3,2,1,0:T(8,128)(2,1)}, u32[]{:S(2)}, u32[]{:S(2)}) %all-to-all-start.1) | async-done | bytes 16777248 | tf_op jit(solution)/shard_map/all_to_all | solution.py:162
  625.4 44.6 %fusion.5 = bf16[1,2,1024,2048]{3,2,1,0:T(8,128)(2,1)} fusion(bf16[1,2,1024,2048]{3,2,1,0:T(8,128)(2,1)} %param.13, bf16[2,1024,4096]{2,1,0:T(8,128)(2,1)} %bitcast.70, bf16[4096,2048,1]{1,0,2:T(8,128)(2,1)} %bitcast.26), kind=kOutput, calls=%fused_computation.11 | convolution fusion | flops 34372321280 | bytes 50331648 | tf_op jit(solution)/shard_map/dot_general | solution.py:89
  (277 shorter events, 248.7 us)
Async XLA Ops:
  1.0 23.1 %collective-permute-start = (bf16[2,32,2048]{2,1,0:T(8,128)(2,1)S(1)}, bf16[2,32,2048]{2,1,0:T(8,128)(2,1)S(1)}, u32[]{:S(2)}, u32[]{:S(2)}) collective-permute-start(bf16[2,32,2048]{2,1,0:T(8,128)(2,1)S(1)} %slice_bitcast_fusion), channel_id=1, source_target_pairs={{0,4},{4,8},{8,12},{12,16},{16,20},{20,24},{24,28},{28,32},{32,36}... | collective-permute-start | bytes 786440 | tf_op jit(solution)/shard_map/ppermute | solution.py:23
  5.7 401.2 %all-to-all-start = ((s32[32,1,2,4]{3,2,1,0:T(2,128)}), s32[32,1,2,4]{3,2,1,0:T(2,128)S(1)}, u32[]{:S(2)}, u32[]{:S(2)}) async-start(s32[32,1,2,4]{3,2,1,0:T(2,128)} %copy.64), calls=%async_computation | async-start | bytes 65536 | tf_op jit(solution)/shard_map/all_to_all | solution.py:163
  18.3 5.1 copy-start
  150.0 5.2 collective-permute-start.1
  151.4 8.3 %collective-permute-start.2 = (bf16[16,2,32,64]{3,2,1,0:T(8,128)(2,1)S(1)}, bf16[16,2,32,64]{3,2,1,0:T(8,128)(2,1)S(1)}, u32[]{:S(2)}, u32[]{:S(2)}) collective-permute-start(bf16[16,2,32,64]{3,2,1,0:T(8,128)(2,1)S(1)} %get-tuple-element.126), channel_id=1, source_target_pairs={{1,0},{2,1},{3,2},{5,4},{6,5},{7,6},{9,8},{10,9},{11,10},{13,12},{... | collective-permute-start | bytes 393224 | tf_op jit(solution)/shard_map/ppermute | solution.py:49
  406.9 218.5 %all-to-all-start.1 = ((bf16[32,1,2,2,32,2048]{5,4,3,2,1,0:T(8,128)(2,1)}), bf16[32,1,2,2,32,2048]{5,4,3,2,1,0:T(8,128)(2,1)}, u32[]{:S(2)}, u32[]{:S(2)}) async-start(bf16[32,1,2,2,32,2048]{5,4,3,2,1,0:T(8,128)(2,1)} %bitcast.69), calls=%async_computation.1 | async-start | bytes 33554432 | tf_op jit(solution)/shard_map/all_to_all | solution.py:162
where the time goes:
time: 682 us; the launch traced here: 670 us
  local copies, waits for them, and re-layouts  273 us (40%)
  waiting for transfers between devices  126 us (18%)
  other arithmetic  101 us (15%)
  blocking collectives  77.3 us (11%)
  matrix products  51.7 us (8%)
  loops' own time  21.6 us (3%)
  starting transfers between devices  18.2 us (3%)
    gather x192, local copies, waits for them, and re-layouts  238 us
    all_to_all x1, waiting for transfers between devices, per_device(): lax.all_to_all(outgoing, 'ping', split_axis=0, concat_axis=0, tiled=True)  121 us
    another operation x3, other arithmetic  85.4 us
    all_gather x1, blocking collectives, prefix(): everything = lax.all_gather(shard, axis)  65.6 us
    dot_general x1, matrix products, focus_tile(): jnp.dot(weights, flat_rows.reshape(-1, block_len), preferred_element_type...  44.6 us
    another operation x1, loops' own time, prefix(): return lax.fori_loop(0, length, step, start)  21.5 us
    dynamic_slice x32, local copies, waits for them, and re-layouts, step(): new = combine(before, everything[k])  18.8 us
  transfers between devices with their start and end apart: 5, of which 3 were waited for; matrix products, arithmetic and copies ran while one was open for 57% of the time, Pallas kernels for 0%

commit v1 on v0

v1 whole, which is shorter than its diff:
```python
import functools
import math

import jax
import jax.numpy as jnp
from jax import lax
from jax.experimental import pallas as pl
from jax.experimental.pallas import tpu as pltpu
from jax.sharding import PartitionSpec as P

C = 32
X = 1024
BAND = 64
MOST = 48
PING_DEV = 16
SPACING = X // PING_DEV
CAP = 2
EDGE = 128

phase_modulus = 4099
small_value = 1e-06


def window_kernel(table, echo_ref, left_ref, right_ref, out_ref):
    slot = pl.program_id(0)
    local = table[0, slot]
    offset = table[1, slot]
    live = table[2, slot]

    @pl.when(live == 0)
    def _():
        out_ref[...] = jnp.zeros_like(out_ref)

    @pl.when(live != 0)
    def _():
        tiles = echo_ref.shape[2] // 128
        rows = echo_ref.shape[1]
        back = jnp.where(offset < 0, 1, 0)
        rem = offset + 128 * back
        turn = lax.rem(128 - rem, 128)
        lane = lax.broadcasted_iota(jnp.int32, (rows, 128), 1)
        keep = lane < 128 - rem
        left = left_ref[local].astype(jnp.float32)
        right = right_ref[local].astype(jnp.float32)
        first = echo_ref[local, :, 0:128].astype(jnp.float32)
        current = pltpu.roll(jnp.where(back == 1, left, first), turn, 1)
        for k in range(tiles):
            ahead = (
                echo_ref[local, :, 128 * (k + 1) : 128 * (k + 2)].astype(jnp.float32)
                if k + 1 < tiles
                else right
            )
            here = echo_ref[local, :, 128 * k : 128 * (k + 1)].astype(jnp.float32)
            following = pltpu.roll(jnp.where(back == 1, here, ahead), turn, 1)
            out_ref[0, :, 128 * k : 128 * (k + 1)] = jnp.where(keep, current, following).astype(
                jnp.bfloat16
            )
            current = following


def cut_windows(table, echoes, left, right):
    pings, rows, length = echoes.shape
    slots = table.shape[1]
    whole = lambda i, t: (0, 0, 0)
    return pl.pallas_call(
        window_kernel,
        out_shape=jax.ShapeDtypeStruct((slots, rows, length), jnp.bfloat16),
        grid_spec=pltpu.PrefetchScalarGridSpec(
            num_scalar_prefetch=1,
            grid=(slots,),
            in_specs=[
                pl.BlockSpec((pings, rows, length), whole),
                pl.BlockSpec((pings, rows, EDGE), whole),
                pl.BlockSpec((pings, rows, EDGE), whole),
            ],
            out_specs=pl.BlockSpec((1, rows, length), lambda i, t: (i, 0, 0)),
        ),
        cost_estimate=pl.CostEstimate(flops=0, bytes_accessed=20 << 20, transcendentals=0),
    )(table, echoes, left, right)


def weight_kernel(cos_ref, sin_ref, out_ref):
    width = cos_ref.shape[2]

    def spread(row):
        return pltpu.roll(
            jnp.broadcast_to(row, (C, width)), width - 2 * (C - 1), 1, stride=2, stride_axis=0
        )[:, :X]

    upper, lower = [], []
    for s in range(2):
        cosine = spread(cos_ref[0, s : s + 1, :])
        sine = spread(sin_ref[0, s : s + 1, :])
        upper += [cosine, -sine]
        lower += [sine, cosine]
    out_ref[0] = jnp.concatenate(upper, axis=0).T.astype(jnp.bfloat16)
    out_ref[1] = jnp.concatenate(lower, axis=0).T.astype(jnp.bfloat16)


def spread_weights(cosine, sine):
    slots, width = cosine.shape
    pairs = slots // 2
    block = pl.BlockSpec((1, 2, width), lambda i: (i, 0, 0))
    return pl.pallas_call(
        weight_kernel,
        out_shape=jax.ShapeDtypeStruct((2, X, slots * 2 * C), jnp.bfloat16),
        grid=(pairs,),
        in_specs=[block, block],
        out_specs=pl.BlockSpec((2, X, 4 * C), lambda i: (0, 0, i)),
        cost_estimate=pl.CostEstimate(flops=0, bytes_accessed=16 << 20, transcendentals=0),
    )(cosine.reshape(pairs, 2, width), sine.reshape(pairs, 2, width))


def per_device(echoes, pairing, footprint, counts, offsets, earlier):
    ping_dev = echoes.shape[0]
    block_len = echoes.shape[3]
    owners = lax.axis_size("ping")
    own_index = lax.axis_index("ping")
    rng_size = lax.axis_size("rng")
    flat = echoes.reshape(ping_dev, 2 * C, block_len)

    left = lax.ppermute(
        flat[:, :, block_len - EDGE :], "rng", [(i, i + 1) for i in range(rng_size - 1)]
    )
    right = lax.ppermute(flat[:, :, :EDGE], "rng", [(i + 1, i) for i in range(rng_size - 1)])

    positions = jnp.arange(MOST, dtype=jnp.int32)
    in_list = positions[None, :] < counts[:, None]
    owner_of = jnp.where(in_list, footprint // ping_dev, -1)
    earlier_same = jnp.sum(
        (
            (owner_of[:, None, :] == owner_of[:, :, None])
            & (positions[None, :] < positions[:, None])[None]
        ).astype(jnp.int32),
        axis=2,
    )
    slot_ids = jnp.arange(CAP, dtype=jnp.int32)

    mine = (owner_of == own_index)[:, None, :] & (earlier_same[:, None, :] == slot_ids[None, :, None])
    mine = mine.astype(jnp.int32)
    table = jnp.stack(
        [
            jnp.sum(mine * (footprint % ping_dev)[:, None, :], axis=2).reshape(-1),
            jnp.sum(mine * offsets[:, None, :], axis=2).reshape(-1),
            jnp.sum(mine, axis=2).reshape(-1),
        ]
    )
    outgoing = cut_windows(table, flat, left, right)
    received = lax.all_to_all(
        outgoing.reshape(owners, CAP, 2 * C, block_len), "ping", split_axis=0, concat_axis=0, tiled=True
    )

    channel_ids = jnp.arange(C, dtype=jnp.int32)
    front_pick = (pairing[:, 0, :, None] == channel_ids).astype(jnp.bfloat16)
    rear_pick = (pairing[:, 1, :, None] == channel_ids).astype(jnp.bfloat16)
    rear_rows = jnp.einsum("pkc,pzcr->pzkr", rear_pick, echoes, preferred_element_type=jnp.float32)
    inner_rows = jnp.einsum(
        "pkc,pzcr->pzkr", front_pick[1:], echoes[:-1], preferred_element_type=jnp.float32
    )
    last_ping = lax.ppermute(echoes[-1], "ping", [(i, i + 1) for i in range(owners - 1)])
    lead_rows = jnp.einsum("kc,zcr->zkr", front_pick[0], last_ping, preferred_element_type=jnp.float32)
    front_rows = jnp.concatenate([lead_rows[None], inner_rows], axis=0)
    cross_sum = jnp.sum(
        front_rows[:, 0] * rear_rows[:, 1] - front_rows[:, 1] * rear_rows[:, 0], axis=(1, 2)
    )
    front_energy = jnp.sum(front_rows * front_rows, axis=(1, 2, 3))
    rear_energy = jnp.sum(rear_rows * rear_rows, axis=(1, 2, 3))
    sums = lax.all_gather(jnp.stack([cross_sum, front_energy, rear_energy]), ("ping", "rng"))
    sums = jnp.sum(sums.reshape(owners, rng_size, 3, ping_dev), axis=1)
    increment = sums[:, 0] / (jnp.sqrt(sums[:, 1] * sums[:, 2]) + small_value)
    increment = increment.reshape(-1)
    every = jnp.arange(owners * ping_dev, dtype=jnp.int32)
    track_turn = jnp.sum(
        jnp.where(every[None, :] <= every[:, None], increment[None, :], 0.0), axis=1
    )

    tile_id = own_index
    pick_owner = jnp.arange(owners, dtype=jnp.int32)
    own_owner = lax.dynamic_index_in_dim(owner_of, tile_id, 0, keepdims=False)
    own_rank = lax.dynamic_index_in_dim(earlier_same, tile_id, 0, keepdims=False)
    own_foot = lax.dynamic_index_in_dim(footprint, tile_id, 0, keepdims=False)
    own_offset = lax.dynamic_index_in_dim(offsets, tile_id, 0, keepdims=False)
    own_count = lax.dynamic_index_in_dim(counts, tile_id, 0, keepdims=False)
    held = (own_owner[None, None, :] == pick_owner[:, None, None]) & (
        own_rank[None, None, :] == slot_ids[None, :, None]
    )
    held = held.astype(jnp.int32).reshape(owners * CAP, MOST)
    live = jnp.sum(held, axis=1).astype(jnp.float32)
    ping_ids = jnp.sum(held * own_foot[None, :], axis=1)
    shift_ids = jnp.sum(held * own_offset[None, :], axis=1)
    turn = jnp.sum(jnp.where(every[None, :] == ping_ids[:, None], track_turn[None, :], 0.0), axis=1)

    width = X + 128
    start = tile_id * X - ping_ids * SPACING - 2 * (C - 1)
    along = jnp.arange(width, dtype=jnp.int32)
    folded = jnp.remainder(start[:, None] + along[None, :], phase_modulus)
    square = jnp.remainder(folded * folded, phase_modulus)
    phases = square.astype(jnp.float32) * (2.0 * math.pi / phase_modulus) + (
        shift_ids.astype(jnp.float32) * (math.pi / 4.0) - turn
    )[:, None]
    scales = live / jnp.sqrt(jnp.float32(C) * own_count.astype(jnp.float32))
    weights = spread_weights(jnp.cos(phases) * scales[:, None], jnp.sin(phases) * scales[:, None])

    contribution = jnp.dot(
        weights.reshape(2 * X, -1),
        received.reshape(-1, block_len),
        preferred_element_type=jnp.float32,
    ).reshape(1, 2, X, block_len)
    return (earlier.astype(jnp.float32) + contribution).astype(jnp.bfloat16)


def solution(mesh):
    return jax.shard_map(
        per_device,
        mesh=mesh,
        in_specs=(
            P("ping", None, None, "rng"),
            P("ping", None, None),
            P(),
            P(),
            P(),
            P("ping", None, None, "rng"),
        ),
        out_specs=P("ping", None, None, "rng"),
        check_vma=False,
    )
```

time: 682 us -> 396 us (0.58); the launches traced: 670 us -> 393 us
  local copies, waits for them, and re-layouts: 273 us -> 5.43 us
  blocking collectives: 77.3 us -> 261 us
  waiting for transfers between devices: 126 us -> 1.03 us
  other arithmetic: 101 us -> 11.3 us
  Pallas kernels: 0 us -> 49.6 us
  loops' own time: 21.6 us -> 0 us
    gather x192 -> x0, local copies, waits for them, and re-layouts: 238 us -> none
    all_gather x1, blocking collectives: 65.6 us -> 261 us  [per_device(): lax.all_gather(jnp.stack([cross_sum, front_energy, rear_energy]), ('ping'...]
    all_to_all x2 -> x1, waiting for transfers between devices: 121 us -> 0.01 us  [per_device(): lax.all_to_all(outgoing.reshape(owners, CAP, 2 * C, block_len), 'ping', s...]
    another operation x6 -> x1, other arithmetic: 88 us -> 0.59 us  [per_device(): jnp.stack([jnp.sum(mine * (footprint % ping_dev)[:, None, :], axis=2).res...]
    pallas_call x0 -> x2, Pallas kernels: none -> 49.6 us  [the longest x1 28 us: cut_windows(): pl.pallas_call(window_kernel, out_shape=jax.ShapeDtypeStruct((slots, rows...]
    another operation x2 -> x0, loops' own time: 21.6 us -> none  [the longest x1 21.5 us: prefix(): return lax.fori_loop(0, length, step, start)]
    dynamic_slice x32 -> x1, local copies, waits for them, and re-layouts: 18.8 us -> 0.59 us  [per_device(): own_count = lax.dynamic_index_in_dim(counts, tile_id, 0, keepdims=False)]
    psum x1 -> x0, blocking collectives: 11.8 us -> none  [per_device(): lax.psum((cross_sum, front_energy, rear_energy), 'rng')]
  transfers between devices with their start and end apart: 5 -> 4, of which waited for: 3 -> 1; matrix products, arithmetic and copies ran while one was open for 57% -> 5% of each run, Pallas kernels for 0% -> 5%
where the time goes in v1:
time: 396 us; the launch traced here: 393 us
  blocking collectives  261 us (66%)
  Pallas kernels  49.6 us (13%)
  matrix products  48.6 us (12%)
  starting transfers between devices  15.6 us (4%)
  other arithmetic  11.3 us (3%)
  local copies, waits for them, and re-layouts  5.43 us (1%)
    all_gather x1, blocking collectives, per_device(): lax.all_gather(jnp.stack([cross_sum, front_energy, rear_energy]), ('ping'...  261 us
    dot_general x1, matrix products, per_device(): jnp.dot(weights.reshape(2 * X, -1), received.reshape(-1, block_len), pref...  44.6 us
    pallas_call x1, Pallas kernels, cut_windows(): pl.pallas_call(window_kernel, out_shape=jax.ShapeDtypeStruct((slots, rows...  28 us
    pallas_call x1, Pallas kernels, spread_weights(): pl.pallas_call(weight_kernel, out_shape=jax.ShapeDtypeStruct((2, X, slots...  21.6 us
  transfers between devices with their start and end apart: 4, of which 1 were waited for; matrix products, arithmetic and copies ran while one was open for 5% of the time, Pallas kernels for 5%

profile of v1, /device:TPU:0, one launch (start us, length us, event | category | flops | bytes accessed | tf_op | source)
XLA Modules:
  0.0 392.8 jit_solution(4953204960056296086)
XLA Ops:
  0.0 1.1 fusion.41
  1.1 1.3 collective-permute-start.2
  2.4 4.6 %collective-permute-start.1 = (bf16[16,64,128]{2,1,0:T(8,128)(2,1)S(1)}, bf16[16,64,128]{2,1,0:T(8,128)(2,1)S(1)}, u32[]{:S(2)}, u32[]{:S(2)}) collective-permute-start(bf16[16,64,128]{2,1,0:T(8,128)(2,1)S(1)} %get-tuple-element.14), channel_id=1, source_target_pairs={{0,1},{1,2},{2,3},{4,5},{5,6},{6,7},{8,9},{9,10},{10,11},{12,13},{... | collective-permute-start | bytes 786440 | tf_op jit(solution)/shard_map/ppermute | solution.py:122
  7.0 0.7 add_select_fusion.2
  7.7 0.8 broadcast_compare_fusion
  8.5 0.8 convert_reduce_fusion
  9.4 0.9 select_reduce_fusion.3
  10.9 0.6 pad_add_fusion.table
  11.5 1.0 collective-permute-done.1.left_ref
  12.5 0.7 copy-done.2
  13.2 28.0 %shard_map.65 = bf16[64,64,2048]{2,1,0:T(8,128)(2,1)} custom-call(s32[3,64]{1,0:T(4,128)} %pad_add_fusion.table, bf16[16,64,2048]{2,1,0:T(8,128)(2,1)} %bitcast.61, bf16[16,64,128]{2,1,0:T(8,128)(2,1)} %copy-done.2, bf16[16,64,128]{2,1,0:T(8,128)(2,1)} %copy-done.1), custom_call_target="tpu_custom_call" | custom-call | bytes 20971520 | tf_op jit(solution)/shard_map/pallas_call | solution.py:65
  41.2 7.6 %all-to-all-start = ((bf16[32,2,64,2048]{3,2,1,0:T(8,128)(2,1)}), bf16[32,2,64,2048]{3,2,1,0:T(8,128)(2,1)}, u32[]{:S(2)}, u32[]{:S(2)}) async-start(bf16[32,2,64,2048]{3,2,1,0:T(8,128)(2,1)} %bitcast.59), calls=%async_computation | async-start | bytes 33554432 | tf_op jit(solution)/shard_map/all_to_all | solution.py:149
  48.8 1.0 slice_bitcast_fusion
  49.7 2.1 collective-permute-start
  51.9 0.6 dynamic_slice.24
  53.3 0.7 fusion.38
  54.7 3.2 multiply_reduce_fusion
  57.8 0.4 fusion.16
  58.2 0.6 fusion.3
  59.3 0.3 fusion.11
  59.6 260.5 %all-gather.1 = f32[128,3,16]{2,1,0:T(4,128)S(1)} all-gather(f32[1,3,16]{2,1,0:T(4,128)S(1)} %maximum_bitcast_fusion), channel_id=2, replica_groups=mesh['ping'=32,'rng'=4] {'ping','rng'}, dimensions={0}, use_global_device_ids=true | all-gather | bytes 24768 | tf_op jit(solution)/shard_map/all_gather | solution.py:168
  321.0 5.6 %sine_multiply_fusion = (f32[32,2,1152]{2,1,0:T(2,128)}, f32[32,2,1152]{2,1,0:T(2,128)}) fusion(f32[32,2]{1,0:T(8,128)S(1)} %copy.29, f32[32,2]{1,0:T(8,128)S(1)} %copy.28, f32[32,2,1152]{2,0,1:T(8,128)S(1)} %fusion.16), kind=kLoop, calls=%fused_computation.31 | loop fusion | flops 294912 | bytes 885248 | tf_op jit(solution)/shard_map/mul | solution.py:202
  326.6 21.6 %shard_map.64 = bf16[2,1024,4096]{2,1,0:T(8,128)(2,1)} custom-call(f32[32,2,1152]{2,1,0:T(2,128)} %get-tuple-element.16.cos_ref, f32[32,2,1152]{2,1,0:T(2,128)} %get-tuple-element.15.sin_ref), custom_call_target="tpu_custom_call" | custom-call | bytes 16777216 | tf_op jit(solution)/shard_map/pallas_call | solution.py:104
  348.2 44.6 %fusion = bf16[1,2,1024,2048]{3,2,1,0:T(8,128)(2,1)} fusion(bf16[1,2,1024,2048]{3,2,1,0:T(8,128)(2,1)} %param.11, bf16[2,1024,4096]{2,1,0:T(8,128)(2,1)} %shard_map.64, bf16[4096,2048,1]{1,0,2:T(8,128)(2,1)} %bitcast.26), kind=kOutput, calls=%fused_computation.1 | convolution fusion | flops 34372321280 | bytes 50331648 | tf_op jit(solution)/shard_map/dot_general | solution.py:204
  (44 shorter events, 2.7 us)
Async XLA Ops:
  1.1 10.4 %collective-permute-start.2 = (bf16[16,64,128]{2,1,0:T(8,128)(2,1)S(1)}, bf16[16,64,128]{2,1,0:T(8,128)(2,1)S(1)}, u32[]{:S(2)}, u32[]{:S(2)}) collective-permute-start(bf16[16,64,128]{2,1,0:T(8,128)(2,1)S(1)} %get-tuple-element.13), channel_id=1, source_target_pairs={{1,0},{2,1},{3,2},{5,4},{6,5},{7,6},{9,8},{10,9},{11,10},{13,12},{... | collective-permute-start | bytes 786440 | tf_op jit(solution)/shard_map/ppermute | solution.py:125
  2.4 10.1 %collective-permute-start.1 = (bf16[16,64,128]{2,1,0:T(8,128)(2,1)S(1)}, bf16[16,64,128]{2,1,0:T(8,128)(2,1)S(1)}, u32[]{:S(2)}, u32[]{:S(2)}) collective-permute-start(bf16[16,64,128]{2,1,0:T(8,128)(2,1)S(1)} %get-tuple-element.14), channel_id=1, source_target_pairs={{0,1},{1,2},{2,3},{4,5},{5,6},{6,7},{8,9},{9,10},{10,11},{12,13},{... | collective-permute-start | bytes 786440 | tf_op jit(solution)/shard_map/ppermute | solution.py:122
  11.5 1.0 copy-start.1
  12.5 0.7 copy-start.2
  41.2 10.7 %copy-start.4 = (s32[32]{0:T(128)S(1)}, s32[32]{0:T(128)}, u32[]{:S(2)}) copy-start(s32[32]{0:T(128)} %param.9) | copy-start | bytes 388
  41.2 12.0 %copy-start.3 = (s32[16,2,8]{0,2,1:T(8,128)S(1)}, s32[16,2,8]{0,2,1:T(8,128)}, u32[]{:S(2)}) copy-start(s32[16,2,8]{0,2,1:T(8,128)} %param.7) | copy-start | bytes 3076
  41.2 307.0 %all-to-all-start = ((bf16[32,2,64,2048]{3,2,1,0:T(8,128)(2,1)}), bf16[32,2,64,2048]{3,2,1,0:T(8,128)(2,1)}, u32[]{:S(2)}, u32[]{:S(2)}) async-start(bf16[32,2,64,2048]{3,2,1,0:T(8,128)(2,1)} %bitcast.59), calls=%async_computation | async-start | bytes 33554432 | tf_op jit(solution)/shard_map/all_to_all | solution.py:149
  49.7 9.1 %collective-permute-start = (bf16[2,32,2048]{2,1,0:T(8,128)(2,1)S(1)}, bf16[2,32,2048]{2,1,0:T(8,128)(2,1)S(1)}, u32[]{:S(2)}, u32[]{:S(2)}) collective-permute-start(bf16[2,32,2048]{2,1,0:T(8,128)(2,1)S(1)} %slice_bitcast_fusion), channel_id=1, source_target_pairs={{0,4},{4,8},{8,12},{12,16},{16,20},{20,24},{24,28},{28,32},{32,36}... | collective-permute-start | bytes 786440 | tf_op jit(solution)/shard_map/ppermute | solution.py:160
  54.6 3.7 copy-start

commit v2 on v1

v2 whole, which is shorter than its diff:
```python
import functools
import math

import jax
import jax.numpy as jnp
from jax import lax
from jax.experimental import pallas as pl
from jax.experimental.pallas import tpu as pltpu
from jax.sharding import PartitionSpec as P

C = 32
X = 1024
MOST = 48
PING_DEV = 16
SPACING = X // PING_DEV
SIDE = 4
CORES = 2
HOLD = 8
MESH = pl.DeviceIdType.MESH
ANY = pl.BlockSpec(memory_space=pl.ANY)
IN_VMEM = pl.BlockSpec(memory_space=pltpu.VMEM)

phase_modulus = 4099
small_value = 1e-06


def place(index):
    return index // (SIDE * CORES), (index // CORES) % SIDE, index % CORES


def device(y, x, c):
    return (((y + SIDE) % SIDE) * SIDE + (x + SIDE) % SIDE) * CORES + (c + CORES) % CORES


def gather_kernel(
    rng_size,
    echo_ref,
    front_ref,
    rear_ref,
    row_ref,
    column_ref,
    row_edge_ref,
    column_edge_ref,
    sums_ref,
    held,
    beside,
    edges,
    partial,
    total,
    local_sem,
    send_sem,
    recv_sem,
    sum_send,
    sum_recv,
):
    me = lax.axis_index("ping")
    level = lax.axis_index("rng")
    y, x, c = place(me)
    owners = SIDE * SIDE * CORES
    pings, half = PING_DEV, PING_DEV // 2
    length = echo_ref.shape[3]

    barrier = pltpu.get_barrier_semaphore()
    for step in range(1, owners):
        pl.semaphore_signal(
            barrier, inc=1, device_id={"ping": (me + step) % owners}, device_id_type=MESH
        )
    for step in range(1, rng_size):
        pl.semaphore_signal(
            barrier, inc=1, device_id={"rng": (level + step) % rng_size}, device_id_type=MESH
        )
    own = pltpu.make_async_copy(echo_ref, held.at[pl.ds(1, pings)], local_sem.at[0])
    own.start()
    pl.semaphore_wait(barrier, owners + rng_size - 2)

    started = []

    def send(src, dst, target):
        i = len(started)
        copy = pltpu.make_async_remote_copy(
            src_ref=src,
            dst_ref=dst,
            send_sem=send_sem.at[i],
            recv_sem=recv_sem.at[i],
            device_id=target,
            device_id_type=MESH,
        )
        copy.start()
        started.append(copy)
        return copy

    up, down = {"rng": (level + 1) % rng_size}, {"rng": (level + rng_size - 1) % rng_size}
    ahead = {"ping": device(y, x + 1, c)}
    behind = {"ping": device(y, x - 1, c)}
    above = {"ping": device(y + 1, x, c)}
    below = {"ping": device(y - 1, x, c)}
    lead = send(echo_ref.at[pings - 1], held.at[0], {"ping": (me + 1) % owners})
    from_low = send(echo_ref.at[:, :, :, pl.ds(length - 128, 128)], beside.at[0], up)
    from_high = send(echo_ref.at[:, :, :, pl.ds(0, 128)], beside.at[1], down)
    low, high = pl.ds(0, half), pl.ds(half, half)
    row_forward = [
        send(echo_ref.at[part, 0], row_ref.at[2, part], ahead) for part in (low,)
    ]
    row_backward = [send(echo_ref.at[high, 0], row_ref.at[0, high], behind)]
    column_forward = [send(echo_ref.at[low, 1], column_ref.at[2, low], above)]
    column_backward = [send(echo_ref.at[high, 1], column_ref.at[0, high], below)]
    row_forward.append(send(echo_ref.at[high, 0], row_ref.at[2, high], ahead))
    row_backward.append(send(echo_ref.at[low, 0], row_ref.at[0, low], behind))
    column_forward.append(send(echo_ref.at[high, 1], column_ref.at[2, high], above))
    column_backward.append(send(echo_ref.at[low, 1], column_ref.at[0, low], below))

    from_low.wait_recv()
    from_high.wait_recv()
    lane = lax.broadcasted_iota(jnp.int32, (C, 128), 1)
    use_low = level > 0
    use_high = level < rng_size - 1

    def merge(p, carry):
        for part in range(2):
            low_edge = beside[0, p, part].astype(jnp.float32)
            high_edge = beside[1, p, part].astype(jnp.float32)
            merged = jnp.where(
                lane < 64,
                jnp.where(use_high, high_edge, 0.0),
                jnp.where(use_low, low_edge, 0.0),
            )
            edges[part, p] = merged.astype(jnp.bfloat16)
        return carry

    lax.fori_loop(0, pings, merge, 0)
    row_edges = [
        send(edges.at[0], row_edge_ref.at[3], ahead),
        send(edges.at[0], row_edge_ref.at[1], behind),
    ]
    column_edges = [
        send(edges.at[1], column_edge_ref.at[3], above),
        send(edges.at[1], column_edge_ref.at[1], below),
    ]
    own_edges = [
        pltpu.make_async_copy(edges.at[0], row_edge_ref.at[0], local_sem.at[1]),
        pltpu.make_async_copy(edges.at[1], column_edge_ref.at[0], local_sem.at[2]),
    ]
    for copy in own_edges:
        copy.start()

    own.wait()
    lead.wait_recv()
    first = (me > 0).astype(jnp.float32)
    place_lane = lax.broadcasted_iota(jnp.int32, (8, 128), 1)

    def fold(value):
        out = value[:, 0:128]
        for k in range(1, length // 128):
            out = out + value[:, 128 * k : 128 * (k + 1)]
        out = jnp.sum(out, axis=0, keepdims=True)
        return jnp.sum(out, axis=1, keepdims=True)

    def correlate(p, acc):
        front, rear = front_ref[p], rear_ref[p]
        scale = jnp.where(p == 0, first, 1.0)
        dot = functools.partial(jnp.dot, preferred_element_type=jnp.float32)
        front_real = dot(front, held[p, 0]) * scale
        front_imag = dot(front, held[p, 1]) * scale
        rear_real = dot(rear, held[p + 1, 0])
        rear_imag = dot(rear, held[p + 1, 1])
        acc = jnp.where(place_lane == p, fold(front_real * rear_imag - front_imag * rear_real), acc)
        acc = jnp.where(
            place_lane == p + pings, fold(front_real * front_real + front_imag * front_imag), acc
        )
        return jnp.where(
            place_lane == p + 2 * pings, fold(rear_real * rear_real + rear_imag * rear_imag), acc
        )

    mine = lax.fori_loop(0, pings, correlate, jnp.zeros((8, 128), jnp.float32))
    partial[0] = mine
    across = []
    for step in range(1, rng_size):
        across.append(
            pltpu.make_async_remote_copy(
                src_ref=partial.at[0],
                dst_ref=partial.at[step],
                send_sem=sum_send.at[owners + step],
                recv_sem=sum_recv.at[owners + step],
                device_id={"rng": (level + step) % rng_size},
                device_id_type=MESH,
            )
        )
        across[-1].start()
    for copy in across:
        copy.wait_recv()
    whole = mine
    for step in range(1, rng_size):
        whole = whole + partial[step]
    total[...] = whole
    own_total = pltpu.make_async_copy(total, sums_ref.at[me], local_sem.at[3])
    own_total.start()
    spread = []
    for step in range(1, owners):
        spread.append(
            pltpu.make_async_remote_copy(
                src_ref=total,
                dst_ref=sums_ref.at[me],
                send_sem=sum_send.at[step],
                recv_sem=sum_recv.at[step],
                device_id={"ping": (me + step) % owners},
                device_id_type=MESH,
            )
        )
        spread[-1].start()

    relays = []
    row_forward[0].wait_recv()
    relays.append(send(row_ref.at[2, low], row_ref.at[1, low], ahead))
    row_backward[0].wait_recv()
    relays.append(send(row_ref.at[0, high], row_ref.at[1, high], behind))
    column_forward[0].wait_recv()
    relays.append(send(column_ref.at[2, low], column_ref.at[1, low], above))
    column_backward[0].wait_recv()
    relays.append(send(column_ref.at[0, high], column_ref.at[1, high], below))
    for copies, out, forth, back in (
        (row_edges, row_edge_ref, ahead, behind),
        (column_edges, column_edge_ref, above, below),
    ):
        copies[0].wait_recv()
        relays.append(send(out.at[3, low], out.at[2, low], forth))
        copies[1].wait_recv()
        relays.append(send(out.at[1, high], out.at[2, high], back))
    for copies in (row_forward, row_backward, column_forward, column_backward):
        copies[1].wait_recv()
    for copy in relays:
        copy.wait_recv()
    for copy in spread:
        copy.wait_recv()
    for copy in started + spread + across:
        copy.wait_send()
    for copy in own_edges:
        copy.wait()
    own_total.wait()


def gather_pings(echoes, front_pick, rear_pick, rng_size):
    pings, parts, channels, length = echoes.shape
    owners = SIDE * SIDE * CORES
    block = (pings, channels, length)
    edge = (pings, channels, 128)
    bf16 = jnp.bfloat16
    copies = 3 + 8 + 4 + 8
    return pl.pallas_call(
        functools.partial(gather_kernel, rng_size),
        out_shape=(
            jax.ShapeDtypeStruct((SIDE - 1,) + block, bf16),
            jax.ShapeDtypeStruct((SIDE - 1,) + block, bf16),
            jax.ShapeDtypeStruct((SIDE,) + edge, bf16),
            jax.ShapeDtypeStruct((SIDE,) + edge, bf16),
            jax.ShapeDtypeStruct((owners, 8, 128), jnp.float32),
        ),
        in_specs=[ANY, IN_VMEM, IN_VMEM],
        out_specs=(ANY,) * 5,
        scratch_shapes=[
            pltpu.VMEM((pings + 1, parts, channels, length), bf16),
            pltpu.VMEM((2, pings, parts, channels, 128), bf16),
            pltpu.VMEM((parts,) + edge, bf16),
            pltpu.VMEM((rng_size, 8, 128), jnp.float32),
            pltpu.VMEM((8, 128), jnp.float32),
            pltpu.SemaphoreType.DMA((4,)),
            pltpu.SemaphoreType.DMA((copies,)),
            pltpu.SemaphoreType.DMA((copies,)),
            pltpu.SemaphoreType.DMA((owners + rng_size,)),
            pltpu.SemaphoreType.DMA((owners + rng_size,)),
        ],
        compiler_params=pltpu.CompilerParams(collective_id=0, has_side_effects=True),
        name="gather_pings",
    )(echoes, front_pick, rear_pick)


def window_kernel(table, echo_ref, row_ref, column_ref, row_edge_ref, column_edge_ref, out_ref, held, edge, sem):
    step = pl.program_id(0)
    pings, length = PING_DEV, held.shape[3]
    tiles = length // 128

    @pl.when(step == 0)
    def _():
        copies = []
        for part, gathered, gathered_edge in ((0, row_ref, row_edge_ref), (1, column_ref, column_edge_ref)):
            copies.append(pltpu.make_async_copy(echo_ref.at[:, part], held.at[part, 0:pings], sem.at[part, 0]))
            for d in range(1, SIDE):
                copies.append(
                    pltpu.make_async_copy(
                        gathered.at[d - 1], held.at[part, pings * d : pings * (d + 1)], sem.at[part, d]
                    )
                )
            for d in range(SIDE):
                copies.append(
                    pltpu.make_async_copy(
                        gathered_edge.at[d], edge.at[part, pings * d : pings * (d + 1)], sem.at[part, SIDE + d]
                    )
                )
        for copy in copies:
            copy.start()
        for copy in copies:
            copy.wait()

    part = step // HOLD
    lane = lax.broadcasted_iota(jnp.int32, (C, 128), 1)

    def one_slot(s, carry):
        local = table[0, step * HOLD + s]
        offset = table[1, step * HOLD + s]
        live = table[2, step * HOLD + s]

        @pl.when(live != 0)
        def _():
            back = offset < 0
            rem = jnp.where(back, offset + 128, offset)
            turn = lax.rem(128 - rem, 128)
            keep = lane < 128 - rem
            outside = edge[part, local].astype(jnp.float32)
            here = held[part, local, :, 0:128].astype(jnp.float32)
            current = pltpu.roll(jnp.where(back, outside, here), turn, 1)
            for k in range(tiles):
                ahead = (
                    held[part, local, :, 128 * (k + 1) : 128 * (k + 2)].astype(jnp.float32)
                    if k + 1 < tiles
                    else outside
                )
                following = pltpu.roll(jnp.where(back, here, ahead), turn, 1)
                out_ref[0, s, :, 128 * k : 128 * (k + 1)] = jnp.where(keep, current, following).astype(
                    jnp.bfloat16
                )
                current, here = following, ahead

        return carry

    lax.fori_loop(0, HOLD, one_slot, 0)


def cut_windows(table, echoes, row, column, row_edge, column_edge):
    pings, parts, channels, length = echoes.shape
    groups = 2 * HOLD
    return pl.pallas_call(
        window_kernel,
        out_shape=jax.ShapeDtypeStruct((groups, HOLD, channels, length), jnp.bfloat16),
        grid_spec=pltpu.PrefetchScalarGridSpec(
            num_scalar_prefetch=1,
            grid=(groups,),
            in_specs=[ANY] * 5,
            out_specs=pl.BlockSpec((1, HOLD, channels, length), lambda i, t: (i, 0, 0, 0)),
            scratch_shapes=[
                pltpu.VMEM((parts, SIDE * pings, channels, length), jnp.bfloat16),
                pltpu.VMEM((parts, SIDE * pings, channels, 128), jnp.bfloat16),
                pltpu.SemaphoreType.DMA((parts, 2 * SIDE)),
            ],
        ),
        name="cut_windows",
    )(table, echoes, row, column, row_edge, column_edge)


def exchange_kernel(slots_ref, received_ref, local_sem, send_sem, recv_sem):
    me = lax.axis_index("ping")
    y, x, c = place(me)
    targets = []
    for part in range(2):
        for k in range(1, HOLD):
            d, dc = k // CORES, k % CORES
            to = device(y + d, x, c + dc) if part == 0 else device(y, x + d, c + dc)
            targets.append((part * HOLD + k, to))
    barrier = pltpu.get_barrier_semaphore()
    for _, to in targets:
        pl.semaphore_signal(barrier, inc=1, device_id={"ping": to}, device_id_type=MESH)
    own = [
        pltpu.make_async_copy(
            slots_ref.at[part * HOLD], received_ref.at[part * HOLD], local_sem.at[part]
        )
        for part in range(2)
    ]
    for copy in own:
        copy.start()
    pl.semaphore_wait(barrier, len(targets))
    copies = []
    order = sorted(range(len(targets)), key=lambda i: (targets[i][0] % HOLD, targets[i][0]))
    for i in order:
        group, to = targets[i]
        copies.append(
            pltpu.make_async_remote_copy(
                src_ref=slots_ref.at[group],
                dst_ref=received_ref.at[group],
                send_sem=send_sem.at[i],
                recv_sem=recv_sem.at[i],
                device_id={"ping": to},
                device_id_type=MESH,
            )
        )
        copies[-1].start()
    for copy in copies:
        copy.wait()
    for copy in own:
        copy.wait()


def exchange(slots):
    count = 2 * (HOLD - 1)
    return pl.pallas_call(
        exchange_kernel,
        out_shape=jax.ShapeDtypeStruct(slots.shape, slots.dtype),
        in_specs=[ANY],
        out_specs=ANY,
        scratch_shapes=[
            pltpu.SemaphoreType.DMA((2,)),
            pltpu.SemaphoreType.DMA((count,)),
            pltpu.SemaphoreType.DMA((count,)),
        ],
        compiler_params=pltpu.CompilerParams(collective_id=1, has_side_effects=True),
        name="exchange",
    )(slots)


def weight_kernel(cos_ref, sin_ref, out_ref):
    width = cos_ref.shape[2]

    def spread(row):
        return pltpu.roll(
            jnp.broadcast_to(row, (C, width)), width - 2 * (C - 1), 1, stride=2, stride_axis=0
        )[:, :X]

    upper, lower = [], []
    for s in range(2):
        cosine = spread(cos_ref[0, s : s + 1, :])
        sine = spread(sin_ref[0, s : s + 1, :])
        upper += [cosine, -sine]
        lower += [sine, cosine]
    out_ref[0] = jnp.concatenate(upper, axis=0).T.astype(jnp.bfloat16)
    out_ref[1] = jnp.concatenate(lower, axis=0).T.astype(jnp.bfloat16)


def spread_weights(cosine, sine):
    slots, width = cosine.shape
    pairs = slots // 2
    block = pl.BlockSpec((1, 2, width), lambda i: (i, 0, 0))
    return pl.pallas_call(
        weight_kernel,
        out_shape=jax.ShapeDtypeStruct((2, X, slots * 2 * C), jnp.bfloat16),
        grid=(pairs,),
        in_specs=[block, block],
        out_specs=pl.BlockSpec((2, X, 4 * C), lambda i: (0, 0, i)),
        name="spread_weights",
    )(cosine.reshape(pairs, 2, width), sine.reshape(pairs, 2, width))


def focus_kernel(table, weight_ref, real_ref, imag_ref, earlier_ref, out_ref, stacked):
    rows = 256

    def fill(j, carry):
        for part, source in ((0, real_ref), (1, imag_ref)):
            slot = table[part, j]
            at = pl.multiple_of(j * 2 * C + part * C, C)
            stacked[pl.ds(at, C), :] = source[slot // HOLD, slot % HOLD]
        return carry

    lax.fori_loop(0, MOST, fill, 0)

    def multiply(i, carry):
        at = pl.ds(pl.multiple_of(i * rows, rows), rows)
        product = jnp.dot(weight_ref[at, :], stacked[...], preferred_element_type=jnp.float32)
        out_ref[at, :] = (earlier_ref[at, :].astype(jnp.float32) + product).astype(jnp.bfloat16)
        return carry

    lax.fori_loop(0, 2 * X // rows, multiply, 0)


def focus(table, weights, received, earlier):
    groups, hold, channels, length = received.shape
    wide = 512
    return pl.pallas_call(
        focus_kernel,
        out_shape=jax.ShapeDtypeStruct((2 * X, length), jnp.bfloat16),
        grid_spec=pltpu.PrefetchScalarGridSpec(
            num_scalar_prefetch=1,
            grid=(length // wide,),
            in_specs=[
                pl.BlockSpec(weights.shape, lambda n, t: (0, 0), pipeline_mode=pl.Buffered(1)),
                pl.BlockSpec((HOLD, hold, channels, wide), lambda n, t: (0, 0, 0, n)),
                pl.BlockSpec((HOLD, hold, channels, wide), lambda n, t: (1, 0, 0, n)),
                pl.BlockSpec((2 * X, wide), lambda n, t: (0, n)),
            ],
            out_specs=pl.BlockSpec((2 * X, wide), lambda n, t: (0, n)),
            scratch_shapes=[pltpu.VMEM((MOST * 2 * C, wide), jnp.bfloat16)],
        ),
        name="focus",
    )(table, weights, received, received, earlier)


def rank_in(groups, positions):
    same = (groups[:, None, :] == groups[:, :, None]) & (positions[None, :] < positions[:, None])[None]
    return jnp.sum(same.astype(jnp.int32), axis=2)


def per_device(echoes, pairing, footprint, counts, offsets, earlier):
    block_len = echoes.shape[3]
    owners = lax.axis_size("ping")
    rng_size = lax.axis_size("rng")
    me = lax.axis_index("ping")
    y, x, c = place(me)

    channel_ids = jnp.arange(C, dtype=jnp.int32)
    front_pick = (pairing[:, 0, :, None] == channel_ids).astype(jnp.bfloat16)
    rear_pick = (pairing[:, 1, :, None] == channel_ids).astype(jnp.bfloat16)
    row, column, row_edge, column_edge, sums = gather_pings(echoes, front_pick, rear_pick, rng_size)

    steps = jnp.arange(HOLD, dtype=jnp.int32)
    tiles = jnp.concatenate(
        [
            device(y + steps // CORES, x, c + steps % CORES),
            device(y, x + steps // CORES, c + steps % CORES),
        ]
    )
    all_tiles = jnp.arange(owners, dtype=jnp.int32)
    chosen = (tiles[:, None] == all_tiles[None, :]).astype(jnp.int32)
    positions = jnp.arange(MOST, dtype=jnp.int32)
    foot = jnp.sum(chosen[:, :, None] * footprint[None], axis=1)
    shift = jnp.sum(chosen[:, :, None] * offsets[None], axis=1)
    count = jnp.sum(chosen * counts[None, :], axis=1)
    listed = positions[None, :] < count[:, None]
    oy, ox, oc = place(foot // PING_DEV)
    by_row = steps[:, None] >= 0
    by_row = jnp.concatenate([by_row, ~by_row], axis=0)
    group = jnp.where(listed, jnp.where(by_row, oy, ox) * CORES + oc, -1)
    rank = rank_in(group, positions)
    here = group == jnp.where(by_row, y, x) * CORES + c
    distance = jnp.where(by_row, ox - x + SIDE, oy - y + SIDE) % SIDE
    source = distance * PING_DEV + foot % PING_DEV
    fits = (here[:, None, :] & (rank[:, None, :] == steps[None, :, None])).astype(jnp.int32)
    table = jnp.stack(
        [
            jnp.sum(fits * source[:, None, :], axis=2).reshape(-1),
            jnp.sum(fits * shift[:, None, :], axis=2).reshape(-1),
            jnp.sum(fits, axis=2).reshape(-1),
        ]
    )
    slots = cut_windows(table, echoes, row, column, row_edge, column_edge)
    received = exchange(slots)

    own_group = jnp.stack([group[0], group[HOLD]])
    own_rank = jnp.stack([rank[0], rank[HOLD]])
    own_place = jnp.stack([y, x])[:, None]
    own_distance = (own_place - own_group // CORES + SIDE) % SIDE
    own_core = (c - own_group % CORES + CORES) % CORES
    arrival = jnp.where(listed[0:1], (own_distance * CORES + own_core) * HOLD + own_rank, -1)
    arrival = jnp.where(listed[0:1], arrival, arrival[:, 0:1])

    sums = sums[:, 0, :]
    cross, front, rear = (sums[:, k * PING_DEV : (k + 1) * PING_DEV] for k in range(3))
    increment = (cross / (jnp.sqrt(front * rear) + small_value)).reshape(-1)
    every = jnp.arange(owners * PING_DEV, dtype=jnp.int32)
    track_turn = jnp.sum(jnp.where(every[None, :] <= every[:, None], increment[None, :], 0.0), axis=1)
    turn = jnp.sum(jnp.where(every[None, :] == foot[0][:, None], track_turn[None, :], 0.0), axis=1)

    width = X + 128
    start = me * X - foot[0] * SPACING - 2 * (C - 1)
    along = jnp.arange(width, dtype=jnp.int32)
    folded = jnp.remainder(start[:, None] + along[None, :], phase_modulus)
    square = jnp.remainder(folded * folded, phase_modulus)
    phases = square.astype(jnp.float32) * (2.0 * math.pi / phase_modulus) + (
        shift[0].astype(jnp.float32) * (math.pi / 4.0) - turn
    )[:, None]
    scales = listed[0].astype(jnp.float32) / jnp.sqrt(jnp.float32(C) * count[0].astype(jnp.float32))
    weights = spread_weights(jnp.cos(phases) * scales[:, None], jnp.sin(phases) * scales[:, None])

    image = focus(arrival, weights.reshape(2 * X, -1), received, earlier.reshape(2 * X, block_len))
    return image.reshape(earlier.shape)


def solution(mesh):
    return jax.shard_map(
        per_device,
        mesh=mesh,
        in_specs=(
            P("ping", None, None, "rng"),
            P("ping", None, None),
            P(),
            P(),
            P(),
            P("ping", None, None, "rng"),
        ),
        out_specs=P("ping", None, None, "rng"),
        check_vma=False,
    )
```

time: 396 us -> 278 us (0.70)
  blocking collectives: 261 us -> 0 us
  Pallas kernels: 49.6 us -> 261 us
  matrix products: 48.6 us -> 0 us
  starting transfers between devices: 15.6 us -> 0 us
    all_gather x1 -> x0, blocking collectives: 261 us -> none  [per_device(): lax.all_gather(jnp.stack([cross_sum, front_energy, rear_energy]), ('ping'...]
    pallas_call x1 -> x4, Pallas kernels: 28 us -> 245 us  [the longest x1 96.3 us: exchange(): pl.pallas_call(exchange_kernel, out_shape=jax.ShapeDtypeStruct(slots.shap...]
    dot_general x4 -> x0, matrix products: 48.6 us -> none  [the longest x1 44.6 us: per_device(): jnp.dot(weights.reshape(2 * X, -1), received.reshape(-1, block_len), pref...]
    ppermute x3 -> x0, starting transfers between devices: 7.99 us -> none  [the longest x1 4.58 us: per_device(): lax.ppermute(flat[:, :, block_len - EDGE:], 'rng', [(i, i + 1) for i in r...]
    all_to_all x1 -> x0, starting transfers between devices: 7.58 us -> none  [per_device(): lax.all_to_all(outgoing.reshape(owners, CAP, 2 * C, block_len), 'ping', s...]
    pallas_call x1, Pallas kernels: 21.6 us -> 16.9 us  [spread_weights(): pl.pallas_call(weight_kernel, out_shape=jax.ShapeDtypeStruct((2, X, slots...]
  transfers between devices with their start and end apart: 4 -> 0, of which waited for: 1 -> 0; matrix products, arithmetic and copies ran while one was open for 5% -> 0% of each run, Pallas kernels for 5% -> 0%
where the time goes in v2:
time: 278 us; the launch traced here: 275 us
  Pallas kernels  261 us (94%)
  other arithmetic  10.7 us (4%)
    pallas_call x1, Pallas kernels, exchange(): pl.pallas_call(exchange_kernel, out_shape=jax.ShapeDtypeStruct(slots.shap...  96.3 us
    pallas_call x1, Pallas kernels, gather_pings(): pl.pallas_call(functools.partial(gather_kernel, rng_size), out_shape=(jax...  86 us
    pallas_call x1, Pallas kernels, focus(): pl.pallas_call(focus_kernel, out_shape=jax.ShapeDtypeStruct((2 * X, lengt...  45.2 us
    pallas_call x1, Pallas kernels, cut_windows(): pl.pallas_call(window_kernel, out_shape=jax.ShapeDtypeStruct((groups, HOL...  17 us
    pallas_call x1, Pallas kernels, spread_weights(): pl.pallas_call(weight_kernel, out_shape=jax.ShapeDtypeStruct((2, X, slots...  16.9 us

profile of v2, /device:TPU:0, one launch (start us, length us, event | category | flops | bytes accessed | tf_op | source)
XLA Modules:
  0.0 275.1 jit_solution(13604364936403206801)
XLA Ops:
  0.2 0.9 multiply_reduce_fusion
  1.2 0.8 select_reduce_fusion.4
  2.1 0.5 convert_reduce_fusion
  2.6 0.9 select_reduce_fusion.3
  3.5 0.1 stack_reshape.10
  3.6 0.1 stack_reshape.11
  3.8 0.6 pad_add_fusion.table
  4.4 0.7 slice_bitcast_fusion
  5.2 0.7 fusion.10
  5.9 86.0 %gather_pings.1 = (bf16[3,16,32,2048]{3,2,1,0:T(8,128)(2,1)}, bf16[3,16,32,2048]{3,2,1,0:T(8,128)(2,1)}, bf16[4,16,32,128]{3,2,1,0:T(8,128)(2,1)}, bf16[4,16,32,128]{3,2,1,0:T(8,128)(2,1)}, f32[32,8,128]{2,1,0:T(8,128)}) custom-call(bf16[16,2,32,2048]{3,2,1,0:T(8,128)(2,1)} %echo_ref.3, bf16[16,8,32]{2,1,0:T(8,128)(2,1)} %get-tuple-element.35.front_ref, ...), custom_call_target="tpu_custom_call" | custom-call | tf_op jit(solution)/shard_map/gather_pings/pallas_call | solution.py:248
  91.9 17.0 %cut_windows.1.slots_ref = bf16[16,8,32,2048]{3,2,1,0:T(8,128)(2,1)} custom-call(s32[3,128]{1,0:T(4,128)} %pad_add_fusion.table, bf16[16,2,32,2048]{3,2,1,0:T(8,128)(2,1)} %echo_ref.3, bf16[3,16,32,2048]{3,2,1,0:T(8,128)(2,1)} %get-tuple-element.11.row_ref, bf16[3,16,32,2048]{3,2,1,0:T(8,128)(2,1)} %get-tuple-element.12.column_ref, ...), custom_call_target="tpu_custom_call" | custom-call | tf_op jit(solution)/shard_map/cut_windows/pallas_call | solution.py:340
  108.9 96.3 %exchange.1.real_ref.imag_ref = bf16[16,8,32,2048]{3,2,1,0:T(8,128)(2,1)} custom-call(bf16[16,8,32,2048]{3,2,1,0:T(8,128)(2,1)} %cut_windows.1.slots_ref), custom_call_target="tpu_custom_call" | custom-call | tf_op jit(solution)/shard_map/exchange/pallas_call | solution.py:402
  205.3 0.9 slice.58
  206.2 0.1 fusion.15
  206.3 0.2 select_reduce_fusion
  206.5 0.2 select_reduce_fusion.1
  206.7 0.1 reduce_sum.89
  206.8 0.1 mul.178
  207.1 0.3 fusion.2
  207.6 4.3 %sine_multiply_fusion = (f32[24,2,1152]{2,1,0:T(2,128)}, f32[24,2,1152]{2,1,0:T(2,128)}) fusion(f32[24,2]{1,0:T(8,128)S(1)} %div.100, f32[24,2]{1,0:T(8,128)S(1)} %sub.107, f32[24,2,1152]{2,0,1:T(8,128)S(1)} %fusion.2), kind=kLoop, calls=%fused_computation.12 | loop fusion | flops 221184 | bytes 663936 | tf_op jit(solution)/shard_map/mul | solution.py:566
  212.0 16.9 %spread_weights.1 = bf16[2,1024,3072]{2,1,0:T(8,128)(2,1)} custom-call(f32[24,2,1152]{2,1,0:T(2,128)} %get-tuple-element.23.cos_ref, f32[24,2,1152]{2,1,0:T(2,128)} %get-tuple-element.22.sin_ref), custom_call_target="tpu_custom_call" | custom-call | tf_op jit(solution)/shard_map/spread_weights/pallas_call | solution.py:439
  229.1 0.1 slice_reduce_fusion
  229.2 0.7 broadcast_select_fusion.table
  229.8 45.2 %focus.1 = bf16[2048,2048]{1,0:T(8,128)(2,1)} custom-call(s32[2,48]{1,0:T(2,128)} %broadcast_select_fusion.table, bf16[2048,3072]{1,0:T(8,128)(2,1)} %bitcast.16, bf16[16,8,32,2048]{3,2,1,0:T(8,128)(2,1)} %exchange.1.real_ref.imag_ref, bf16[16,8,32,2048]{3,2,1,0:T(8,128)(2,1)} %exchange.1.real_ref.imag_ref, bf16[2048,2048]{1,0:T(8,128)(2,1)} %bitcast.17), custom_call_target="tpu_custom_call" | custom-call | tf_op jit(solution)/shard_map/focus/pallas_call | solution.py:473
  (25 shorter events, 1.2 us)

commit v3 on v2

--- a/solution.py
+++ b/solution.py
@@ -355,138 +355,204 @@
     )(table, echoes, row, column, row_edge, column_edge)
 
 
-def exchange_kernel(slots_ref, received_ref, local_sem, send_sem, recv_sem):
+def turns_of(sums_ref, owner, local):
+    sums = sums_ref[:, 0, :]
+    owners = sums.shape[0]
+    lane = lax.broadcasted_iota(jnp.int32, (owners, 128), 1)
+    row = lax.broadcasted_iota(jnp.int32, (owners, 128), 0)
+    front = pltpu.roll(sums, 128 - PING_DEV, 1)
+    rear = pltpu.roll(sums, 128 - 2 * PING_DEV, 1)
+    valid = lane < PING_DEV
+    energy = jnp.where(valid, front * rear, 1.0)
+    running = jnp.where(valid, sums / (jnp.sqrt(energy) + small_value), 0.0)
+    step = 1
+    while step < PING_DEV:
+        running = running + jnp.where(lane >= step, pltpu.roll(running, step, 1), 0.0)
+        step *= 2
+    last = jnp.sum(jnp.where(lane == PING_DEV - 1, running, 0.0), axis=1, keepdims=True)
+    before = jnp.broadcast_to(last, (owners, 128))
+    step = 1
+    while step < owners:
+        before = before + jnp.where(row >= step, pltpu.roll(before, step, 0), 0.0)
+        step *= 2
+    before = jnp.where(row >= 1, pltpu.roll(before, 1, 0), 0.0)
+    turn = jnp.where(valid, running + before, 0.0)
+    entries = owner.shape[0]
+    lane = lax.broadcasted_iota(jnp.int32, (entries, 128), 1)
+    at_lane = lane == local
+    picked = jnp.zeros((entries, 128), jnp.float32)
+    for k in range(owners):
+        picked = picked + jnp.where(at_lane & (owner == k), turn[k : k + 1, :], 0.0)
+    return jnp.sum(picked, axis=1, keepdims=True)
+
+
+def focus_kernel(
+    table,
+    slots_ref,
+    sums_ref,
+    list_ref,
+    scale_ref,
+    earlier_ref,
+    out_ref,
+    weights,
+    stacked,
+    image,
+    cosines,
+    sines,
+    local_sem,
+    send_sem,
+    recv_sem,
+    *received,
+):
     me = lax.axis_index("ping")
     y, x, c = place(me)
+    chunks, wide = len(received), stacked.shape[1]
     targets = []
-    for part in range(2):
-        for k in range(1, HOLD):
+    for k in range(1, HOLD):
+        for part in range(2):
             d, dc = k // CORES, k % CORES
             to = device(y + d, x, c + dc) if part == 0 else device(y, x + d, c + dc)
             targets.append((part * HOLD + k, to))
     barrier = pltpu.get_barrier_semaphore()
     for _, to in targets:
         pl.semaphore_signal(barrier, inc=1, device_id={"ping": to}, device_id_type=MESH)
-    own = [
-        pltpu.make_async_copy(
-            slots_ref.at[part * HOLD], received_ref.at[part * HOLD], local_sem.at[part]
-        )
-        for part in range(2)
-    ]
-    for copy in own:
-        copy.start()
+    own, before = [], []
+    for q in range(chunks):
+        for part in range(2):
+            group = part * HOLD
+            own.append(
+                pltpu.make_async_copy(
+                    slots_ref.at[group, :, :, pl.ds(q * wide, wide)],
+                    received[q].at[pl.ds(group * HOLD, HOLD)],
+                    local_sem.at[q, part],
+                )
+            )
+            own[-1].start()
+    for q in range(chunks):
+        before.append(
+            pltpu.make_async_copy(
+                earlier_ref.at[:, pl.ds(q * wide, wide)], image.at[q], local_sem.at[q, 2]
+            )
+        )
+        before[-1].start()
     pl.semaphore_wait(barrier, len(targets))
     copies = []
-    order = sorted(range(len(targets)), key=lambda i: (targets[i][0] % HOLD, targets[i][0]))
-    for i in order:
-        group, to = targets[i]
-        copies.append(
-            pltpu.make_async_remote_copy(
-                src_ref=slots_ref.at[group],
-                dst_ref=received_ref.at[group],
-                send_sem=send_sem.at[i],
-                recv_sem=recv_sem.at[i],
-                device_id={"ping": to},
-                device_id_type=MESH,
+    for q in range(chunks):
+        for i, (group, to) in enumerate(targets):
+            copies.append(
+                pltpu.make_async_remote_copy(
+                    src_ref=slots_ref.at[group, :, :, pl.ds(q * wide, wide)],
+                    dst_ref=received[q].at[pl.ds(group * HOLD, HOLD)],
+                    send_sem=send_sem.at[q, i],
+                    recv_sem=recv_sem.at[q, i],
+                    device_id={"ping": to},
+                    device_id_type=MESH,
+                )
             )
-        )
-        copies[-1].start()
+            copies[-1].start()
+
+    span = cosines.shape[1]
+    along = lax.broadcasted_iota(jnp.int32, (MOST, span), 1)
+    turn = turns_of(sums_ref, list_ref[:, 0:1], list_ref[:, 1:2])
+    folded = list_ref[:, 2:3] + along
+    folded = jnp.where(folded >= phase_modulus, folded - phase_modulus, folded)
+    square = folded * folded
+    square = square - phase_modulus * (
+        square.astype(jnp.float32) * (1.0 / phase_modulus)
+    ).astype(jnp.int32)
+    square = jnp.where(square < 0, square + phase_modulus, square)
+    square = jnp.where(square >= phase_modulus, square - phase_modulus, square)
+    phases = square.astype(jnp.float32) * (2.0 * math.pi / phase_modulus) + (
+        list_ref[:, 3:4].astype(jnp.float32) * (math.pi / 4.0) - turn
+    )
+    cosines[...] = jnp.cos(phases) * scale_ref[:, 0:1]
+    sines[...] = jnp.sin(phases) * scale_ref[:, 0:1]
+
+    def spread(ref, j):
+        return pltpu.roll(
+            jnp.broadcast_to(ref[pl.ds(j, 1), :], (C, span)),
+            span - 2 * (C - 1),
+            1,
+            stride=2,
+            stride_axis=0,
+        )[:, :X]
+
+    def weigh(pair, carry):
+        upper, lower = [], []
+        for s in range(2):
+            cosine = spread(cosines, 2 * pair + s)
+            sine = spread(sines, 2 * pair + s)
+            upper += [cosine, -sine]
+            lower += [sine, cosine]
+        at = pl.ds(pl.multiple_of(pair * 4 * C, 4 * C), 4 * C)
+        weights[0:X, at] = jnp.concatenate(upper, axis=0).T.astype(jnp.bfloat16)
+        weights[X : 2 * X, at] = jnp.concatenate(lower, axis=0).T.astype(jnp.bfloat16)
+        return carry
+
+    lax.fori_loop(0, MOST // 2, weigh, 0)
+
+    rows = X
+    after = []
+    for q in range(chunks):
+        for copy in own[2 * q : 2 * q + 2]:
+            copy.wait()
+        for copy in copies[q * len(targets) : (q + 1) * len(targets)]:
+            copy.wait_recv()
+
+        def fill(j, carry):
+            for part in range(2):
+                at = pl.multiple_of(j * 2 * C + part * C, C)
+                stacked[pl.ds(at, C), :] = received[q][table[part, j]]
+            return carry
+
+        lax.fori_loop(0, MOST, fill, 0)
+        before[q].wait()
+
+        def multiply(i, carry):
+            at = pl.ds(pl.multiple_of(i * rows, rows), rows)
+            product = jnp.dot(weights[at, :], stacked[...], preferred_element_type=jnp.float32)
+            image[q, at, :] = (image[q, at, :].astype(jnp.float32) + product).astype(jnp.bfloat16)
+            return carry
+
+        lax.fori_loop(0, 2 * X // rows, multiply, 0)
+        after.append(
+            pltpu.make_async_copy(
+                image.at[q], out_ref.at[:, pl.ds(q * wide, wide)], local_sem.at[q, 3]
+            )
+        )
+        after[-1].start()
     for copy in copies:
+        copy.wait_send()
+    for copy in after:
         copy.wait()
-    for copy in own:
-        copy.wait()
-
-
-def exchange(slots):
-    count = 2 * (HOLD - 1)
-    return pl.pallas_call(
-        exchange_kernel,
-        out_shape=jax.ShapeDtypeStruct(slots.shape, slots.dtype),
-        in_specs=[ANY],
-        out_specs=ANY,
-        scratch_shapes=[
-            pltpu.SemaphoreType.DMA((2,)),
-            pltpu.SemaphoreType.DMA((count,)),
-            pltpu.SemaphoreType.DMA((count,)),
-        ],
-        compiler_params=pltpu.CompilerParams(collective_id=1, has_side_effects=True),
-        name="exchange",
-    )(slots)
-
-
-def weight_kernel(cos_ref, sin_ref, out_ref):
-    width = cos_ref.shape[2]
-
-    def spread(row):
-        return pltpu.roll(
-            jnp.broadcast_to(row, (C, width)), width - 2 * (C - 1), 1, stride=2, stride_axis=0
-        )[:, :X]
-
-    upper, lower = [], []
-    for s in range(2):
-        cosine = spread(cos_ref[0, s : s + 1, :])
-        sine = spread(sin_ref[0, s : s + 1, :])
-        upper += [cosine, -sine]
-        lower += [sine, cosine]
-    out_ref[0] = jnp.concatenate(upper, axis=0).T.astype(jnp.bfloat16)
-    out_ref[1] = jnp.concatenate(lower, axis=0).T.astype(jnp.bfloat16)
-
-
-def spread_weights(cosine, sine):
-    slots, width = cosine.shape
-    pairs = slots // 2
-    block = pl.BlockSpec((1, 2, width), lambda i: (i, 0, 0))
-    return pl.pallas_call(
-        weight_kernel,
-        out_shape=jax.ShapeDtypeStruct((2, X, slots * 2 * C), jnp.bfloat16),
-        grid=(pairs,),
-        in_specs=[block, block],
-        out_specs=pl.BlockSpec((2, X, 4 * C), lambda i: (0, 0, i)),
-        name="spread_weights",
-    )(cosine.reshape(pairs, 2, width), sine.reshape(pairs, 2, width))
-
-
-def focus_kernel(table, weight_ref, real_ref, imag_ref, earlier_ref, out_ref, stacked):
-    rows = 256
-
-    def fill(j, carry):
-        for part, source in ((0, real_ref), (1, imag_ref)):
-            slot = table[part, j]
-            at = pl.multiple_of(j * 2 * C + part * C, C)
-            stacked[pl.ds(at, C), :] = source[slot // HOLD, slot % HOLD]
-        return carry
-
-    lax.fori_loop(0, MOST, fill, 0)
-
-    def multiply(i, carry):
-        at = pl.ds(pl.multiple_of(i * rows, rows), rows)
-        product = jnp.dot(weight_ref[at, :], stacked[...], preferred_element_type=jnp.float32)
-        out_ref[at, :] = (earlier_ref[at, :].astype(jnp.float32) + product).astype(jnp.bfloat16)
-        return carry
-
-    lax.fori_loop(0, 2 * X // rows, multiply, 0)
-
-
-def focus(table, weights, received, earlier):
-    groups, hold, channels, length = received.shape
-    wide = 512
+
+
+def focus(table, slots, sums, entries, scales, earlier):
+    groups, hold, channels, length = slots.shape
+    chunks = 4
+    wide = length // chunks
+    count = groups - 2
     return pl.pallas_call(
         focus_kernel,
         out_shape=jax.ShapeDtypeStruct((2 * X, length), jnp.bfloat16),
-        grid_spec=pltpu.PrefetchScalarGridSpec(
-            num_scalar_prefetch=1,
-            grid=(length // wide,),
-            in_specs=[
-                pl.BlockSpec(weights.shape, lambda n, t: (0, 0), pipeline_mode=pl.Buffered(1)),
-                pl.BlockSpec((HOLD, hold, channels, wide), lambda n, t: (0, 0, 0, n)),
-                pl.BlockSpec((HOLD, hold, channels, wide), lambda n, t: (1, 0, 0, n)),
-                pl.BlockSpec((2 * X, wide), lambda n, t: (0, n)),
-            ],
-            out_specs=pl.BlockSpec((2 * X, wide), lambda n, t: (0, n)),
-            scratch_shapes=[pltpu.VMEM((MOST * 2 * C, wide), jnp.bfloat16)],
+        in_specs=[pl.BlockSpec(memory_space=pltpu.SMEM), ANY, IN_VMEM, IN_VMEM, IN_VMEM, ANY],
+        out_specs=ANY,
+        scratch_shapes=[
+            pltpu.VMEM((2 * X, MOST * 2 * C), jnp.bfloat16),
+            pltpu.VMEM((MOST * 2 * C, wide), jnp.bfloat16),
+            pltpu.VMEM((chunks, 2 * X, wide), jnp.bfloat16),
+            pltpu.VMEM((MOST, X + 128), jnp.float32),
+            pltpu.VMEM((MOST, X + 128), jnp.float32),
+            pltpu.SemaphoreType.DMA((chunks, 4)),
+            pltpu.SemaphoreType.DMA((chunks, count)),
+            pltpu.SemaphoreType.DMA((chunks, count)),
+        ]
+        + [pltpu.VMEM((groups * hold, channels, wide), jnp.bfloat16)] * chunks,
+        compiler_params=pltpu.CompilerParams(
+            collective_id=1, has_side_effects=True, vmem_limit_bytes=60 << 20
         ),
         name="focus",
-    )(table, weights, received, received, earlier)
+    )(table, slots, sums, entries, scales, earlier)
 
 
 def rank_in(groups, positions):
@@ -537,35 +603,26 @@
         ]
     )
     slots = cut_windows(table, echoes, row, column, row_edge, column_edge)
-    received = exchange(slots)
 
     own_group = jnp.stack([group[0], group[HOLD]])
     own_rank = jnp.stack([rank[0], rank[HOLD]])
     own_place = jnp.stack([y, x])[:, None]
     own_distance = (own_place - own_group // CORES + SIDE) % SIDE
     own_core = (c - own_group % CORES + CORES) % CORES
-    arrival = jnp.where(listed[0:1], (own_distance * CORES + own_core) * HOLD + own_rank, -1)
+    arrival = (own_distance * CORES + own_core) * HOLD + own_rank
     arrival = jnp.where(listed[0:1], arrival, arrival[:, 0:1])
-
-    sums = sums[:, 0, :]
-    cross, front, rear = (sums[:, k * PING_DEV : (k + 1) * PING_DEV] for k in range(3))
-    increment = (cross / (jnp.sqrt(front * rear) + small_value)).reshape(-1)
-    every = jnp.arange(owners * PING_DEV, dtype=jnp.int32)
-    track_turn = jnp.sum(jnp.where(every[None, :] <= every[:, None], increment[None, :], 0.0), axis=1)
-    turn = jnp.sum(jnp.where(every[None, :] == foot[0][:, None], track_turn[None, :], 0.0), axis=1)
-
-    width = X + 128
-    start = me * X - foot[0] * SPACING - 2 * (C - 1)
-    along = jnp.arange(width, dtype=jnp.int32)
-    folded = jnp.remainder(start[:, None] + along[None, :], phase_modulus)
-    square = jnp.remainder(folded * folded, phase_modulus)
-    phases = square.astype(jnp.float32) * (2.0 * math.pi / phase_modulus) + (
-        shift[0].astype(jnp.float32) * (math.pi / 4.0) - turn
-    )[:, None]
+    arrival = arrival + jnp.array([[0], [HOLD * HOLD]], jnp.int32)
+    entries = jnp.stack(
+        [
+            foot[0] // PING_DEV,
+            foot[0] % PING_DEV,
+            jnp.remainder(me * X - foot[0] * SPACING - 2 * (C - 1), phase_modulus),
+            shift[0],
+        ],
+        axis=1,
+    )
     scales = listed[0].astype(jnp.float32) / jnp.sqrt(jnp.float32(C) * count[0].astype(jnp.float32))
-    weights = spread_weights(jnp.cos(phases) * scales[:, None], jnp.sin(phases) * scales[:, None])
-
-    image = focus(arrival, weights.reshape(2 * X, -1), received, earlier.reshape(2 * X, block_len))
+    image = focus(arrival, slots, sums, entries, scales[:, None], earlier.reshape(2 * X, block_len))
     return image.reshape(earlier.shape)
 
 

time: 278 us -> 230 us (0.83)
  Pallas kernels: 261 us -> 212 us
  local copies, waits for them, and re-layouts: 2.69 us -> 11.1 us
  other arithmetic: 10.7 us -> 5.56 us
    pallas_call x2 -> x0, Pallas kernels: 113 us -> none  [the longest x1 96.3 us: exchange(): pl.pallas_call(exchange_kernel, out_shape=jax.ShapeDtypeStruct(slots.shap...]
    pallas_call x1, Pallas kernels: 45.2 us -> 105 us  [focus(): pl.pallas_call(focus_kernel, out_shape=jax.ShapeDtypeStruct((2 * X, lengt...]
    unnamed x0 -> x1, local copies, waits for them, and re-layouts: none -> 8.44 us
    mul x2 -> x0, other arithmetic: 4.36 us -> none  [the longest x1 4.34 us: per_device(): jnp.sin(phases) * scales[:, None]]
    pallas_call x1, Pallas kernels: 17 us -> 20.5 us  [cut_windows(): pl.pallas_call(window_kernel, out_shape=jax.ShapeDtypeStruct((groups, HOL...]
where the time goes in v3:
time: 230 us; the launch traced here: 228 us
  Pallas kernels  212 us (92%)
  local copies, waits for them, and re-layouts  11.1 us (5%)
  other arithmetic  5.56 us (2%)
    pallas_call x1, Pallas kernels, focus(): pl.pallas_call(focus_kernel, out_shape=jax.ShapeDtypeStruct((2 * X, lengt...  105 us
    pallas_call x1, Pallas kernels, gather_pings(): pl.pallas_call(functools.partial(gather_kernel, rng_size), out_shape=(jax...  86 us
    pallas_call x1, Pallas kernels, cut_windows(): pl.pallas_call(window_kernel, out_shape=jax.ShapeDtypeStruct((groups, HOL...  20.5 us
    unnamed x1, local copies, waits for them, and re-layouts  8.44 us

profile of v3, /device:TPU:0, one launch (start us, length us, event | category | flops | bytes accessed | tf_op | source)
XLA Modules:
  0.0 228.4 jit_solution(6556608391035485230)
XLA Ops:
  0.1 0.1 pad_add_fusion.3
  0.1 0.1 fusion.10
  0.2 0.9 multiply_reduce_fusion
  1.1 0.8 select_reduce_fusion.2
  2.0 0.1 broadcast_compare_fusion
  2.1 0.5 convert_reduce_fusion
  2.6 0.1 pad_add_fusion.4
  2.7 0.1 add_add_fusion
  2.8 0.1 slice_reduce_fusion
  2.9 0.6 select_add_fusion.table
  3.5 0.1 fusion.9
  3.6 0.9 select_reduce_fusion.1
  4.5 0.1 stack_reshape.11
  4.6 0.1 stack_reshape.10
  4.7 0.1 stack_reshape.9
  4.8 0.6 pad_add_fusion.table
  5.3 0.7 slice_bitcast_fusion
  6.2 0.7 fusion.1
  6.9 86.0 %gather_pings.1 = (bf16[3,16,32,2048]{3,2,1,0:T(8,128)(2,1)}, bf16[3,16,32,2048]{3,2,1,0:T(8,128)(2,1)}, bf16[4,16,32,128]{3,2,1,0:T(8,128)(2,1)}, bf16[4,16,32,128]{3,2,1,0:T(8,128)(2,1)}, f32[32,8,128]{2,1,0:T(8,128)}) custom-call(bf16[16,2,32,2048]{3,2,1,0:T(8,128)(2,1)} %echo_ref.3, bf16[16,8,32]{2,1,0:T(8,128)(2,1)} %get-tuple-element.34.front_ref, ...), custom_call_target="tpu_custom_call" | custom-call | tf_op jit(solution)/shard_map/gather_pings/pallas_call | solution.py:248
  92.9 20.5 %cut_windows.1.slots_ref = bf16[16,8,32,2048]{3,2,1,0:T(8,128)(2,1)} custom-call(s32[3,128]{1,0:T(4,128)} %pad_add_fusion.table, bf16[16,2,32,2048]{3,2,1,0:T(8,128)(2,1)} %echo_ref.3, bf16[3,16,32,2048]{3,2,1,0:T(8,128)(2,1)} %get-tuple-element.10.row_ref, bf16[3,16,32,2048]{3,2,1,0:T(8,128)(2,1)} %get-tuple-element.11.column_ref, ...), custom_call_target="tpu_custom_call" | custom-call | tf_op jit(solution)/shard_map/cut_windows/pallas_call | solution.py:340
  113.5 0.7 copy.32.list_ref
  114.3 0.7 copy.33.scale_ref
  114.9 105.0 %focus.1 = bf16[2048,2048]{1,0:T(8,128)(2,1)} custom-call(s32[2,48]{1,0:T(2,128)} %select_add_fusion.table, bf16[16,8,32,2048]{3,2,1,0:T(8,128)(2,1)} %cut_windows.1.slots_ref, f32[32,8,128]{2,1,0:T(8,128)} %get-tuple-element.14.sums_ref, s32[48,4]{1,0:T(8,128)} %copy.32.list_ref, f32[48,1]{1,0:T(8,128)} %copy.33.scale_ref, bf16[2048,2048]{1,0:T(8,128)(2,1)} %bitcast.26), custom_call_target="tpu_custom_call" | custom-call | tf_op jit(solution)/shard_map/focus/pallas_call | solution.py:535
  220.0 8.4 %copy.35 = bf16[1,2,1024,2048]{3,2,1,0:T(8,128)(2,1)} copy(bf16[1,2,1024,2048]{3,2,1,0:T(8,128)(2,1)} %bitcast.25) | data formatting | bytes 16777216
  (16 shorter events, 0.2 us)

commit v4 on v0

v4 whole, which is shorter than its diff:
```python
import functools
import math

import jax
import jax.numpy as jnp
from jax import lax
from jax.experimental import pallas as pl
from jax.experimental.pallas import tpu as pltpu
from jax.sharding import PartitionSpec as P

C = 32
X = 1024
MOST = 48
PING_DEV = 16
SPACING = X // PING_DEV
SIDE = 4
CORES = 2
HOLD = 8
MESH = pl.DeviceIdType.MESH
ANY = pl.BlockSpec(memory_space=pl.ANY)
IN_VMEM = pl.BlockSpec(memory_space=pltpu.VMEM)

phase_modulus = 4099
small_value = 1e-06


def place(index):
    return index // (SIDE * CORES), (index // CORES) % SIDE, index % CORES


def device(y, x, c):
    return (((y + SIDE) % SIDE) * SIDE + (x + SIDE) % SIDE) * CORES + (c + CORES) % CORES


def turns_of(sums_ref, owner, local):
    sums = sums_ref[:, 0, :]
    owners = sums.shape[0]
    lane = lax.broadcasted_iota(jnp.int32, (owners, 128), 1)
    row = lax.broadcasted_iota(jnp.int32, (owners, 128), 0)
    front = pltpu.roll(sums, 128 - PING_DEV, 1)
    rear = pltpu.roll(sums, 128 - 2 * PING_DEV, 1)
    valid = lane < PING_DEV
    energy = jnp.where(valid, front * rear, 1.0)
    running = jnp.where(valid, sums / (jnp.sqrt(energy) + small_value), 0.0)
    step = 1
    while step < PING_DEV:
        running = running + jnp.where(lane >= step, pltpu.roll(running, step, 1), 0.0)
        step *= 2
    last = jnp.sum(jnp.where(lane == PING_DEV - 1, running, 0.0), axis=1, keepdims=True)
    before = jnp.broadcast_to(last, (owners, 128))
    step = 1
    while step < owners:
        before = before + jnp.where(row >= step, pltpu.roll(before, step, 0), 0.0)
        step *= 2
    before = jnp.where(row >= 1, pltpu.roll(before, 1, 0), 0.0)
    turn = jnp.where(valid, running + before, 0.0)
    entries = owner.shape[0]
    lane = lax.broadcasted_iota(jnp.int32, (entries, 128), 1)
    at_lane = lane == local
    picked = jnp.zeros((entries, 128), jnp.float32)
    for k in range(owners):
        picked = picked + jnp.where(at_lane & (owner == k), turn[k : k + 1, :], 0.0)
    return jnp.sum(picked, axis=1, keepdims=True)


def image_kernel(
    rng_size,
    table,
    arrival,
    echo_ref,
    front_ref,
    rear_ref,
    list_ref,
    scale_ref,
    earlier_ref,
    out_ref,
    row_pings,
    column_pings,
    row_edges,
    column_edges,
    lead,
    beside,
    partial,
    total,
    sums,
    staging,
    weights,
    stacked,
    image,
    cosines,
    sines,
    local_sem,
    send_sem,
    recv_sem,
    sum_send,
    sum_recv,
    slot_send,
    slot_recv,
    *received,
):
    me = lax.axis_index("ping")
    level = lax.axis_index("rng")
    y, x, c = place(me)
    owners = SIDE * SIDE * CORES
    pings, half = PING_DEV, PING_DEV // 2
    length = echo_ref.shape[3]
    chunks, wide = len(received), stacked.shape[1]

    barrier = pltpu.get_barrier_semaphore()
    for step in range(1, owners):
        pl.semaphore_signal(
            barrier, inc=1, device_id={"ping": (me + step) % owners}, device_id_type=MESH
        )
    for step in range(1, rng_size):
        pl.semaphore_signal(
            barrier, inc=1, device_id={"rng": (level + step) % rng_size}, device_id_type=MESH
        )
    own = [
        pltpu.make_async_copy(echo_ref.at[:, 0], row_pings.at[pl.ds(0, pings)], local_sem.at[0]),
        pltpu.make_async_copy(echo_ref.at[:, 1], column_pings.at[pl.ds(0, pings)], local_sem.at[1]),
    ]
    before = [
        pltpu.make_async_copy(
            earlier_ref.at[:, pl.ds(q * wide, wide)], image.at[q % 2], local_sem.at[2 + q]
        )
        for q in range(chunks)
    ]
    after = [
        pltpu.make_async_copy(
            image.at[q % 2], out_ref.at[:, pl.ds(q * wide, wide)], local_sem.at[2 + chunks + q]
        )
        for q in range(chunks)
    ]
    for copy in own + before[:2]:
        copy.start()
    pl.semaphore_wait(barrier, owners + rng_size - 2)

    started = []

    def send(src, dst, target):
        i = len(started)
        copy = pltpu.make_async_remote_copy(
            src_ref=src,
            dst_ref=dst,
            send_sem=send_sem.at[i],
            recv_sem=recv_sem.at[i],
            device_id=target,
            device_id_type=MESH,
        )
        copy.start()
        started.append(copy)
        return copy

    up, down = {"rng": (level + 1) % rng_size}, {"rng": (level + rng_size - 1) % rng_size}
    ahead = {"ping": device(y, x + 1, c)}
    behind = {"ping": device(y, x - 1, c)}
    above = {"ping": device(y + 1, x, c)}
    below = {"ping": device(y - 1, x, c)}
    low, high = pl.ds(0, half), pl.ds(half, half)

    def part_of(distance, start):
        return pl.ds(distance * pings + start, half)

    from_lead = send(echo_ref.at[pings - 1], lead, {"ping": (me + 1) % owners})
    from_low = send(echo_ref.at[:, :, :, pl.ds(length - 128, 128)], beside.at[0], up)
    from_high = send(echo_ref.at[:, :, :, pl.ds(0, 128)], beside.at[1], down)
    forward, backward = [], []
    for turn in range(2):
        for part, pool, forth, back in (
            (0, row_pings, ahead, behind),
            (1, column_pings, above, below),
        ):
            first, second = (low, high) if turn == 0 else (high, low)
            forward.append(
                send(echo_ref.at[first, part], pool.at[part_of(3, turn * half)], forth)
            )
            backward.append(
                send(echo_ref.at[second, part], pool.at[part_of(1, (1 - turn) * half)], back)
            )

    from_low.wait_recv()
    from_high.wait_recv()
    lane = lax.broadcasted_iota(jnp.int32, (C, 128), 1)
    use_low = level > 0
    use_high = level < rng_size - 1
    pools = (row_pings, column_pings)
    rims = (row_edges, column_edges)

    def merge(p, carry):
        for part in range(2):
            low_edge = beside[0, p, part].astype(jnp.float32)
            high_edge = beside[1, p, part].astype(jnp.float32)
            merged = jnp.where(
                lane < 64,
                jnp.where(use_high, high_edge, 0.0),
                jnp.where(use_low, low_edge, 0.0),
            )
            rims[part][p] = merged.astype(jnp.bfloat16)
        return carry

    lax.fori_loop(0, pings, merge, 0)

    for copy in own:
        copy.wait()
    from_lead.wait_recv()
    place_lane = lax.broadcasted_iota(jnp.int32, (8, 128), 1)

    def fold(value):
        out = value[:, 0:128]
        for k in range(1, length // 128):
            out = out + value[:, 128 * k : 128 * (k + 1)]
        out = jnp.sum(out, axis=0, keepdims=True)
        return jnp.sum(out, axis=1, keepdims=True)

    def correlate(p, front_source, acc):
        front, rear = front_ref[p], rear_ref[p]
        dot = functools.partial(jnp.dot, preferred_element_type=jnp.float32)
        front_real = dot(front, front_source[0])
        front_imag = dot(front, front_source[1])
        rear_real = dot(rear, row_pings[p])
        rear_imag = dot(rear, column_pings[p])
        acc = jnp.where(place_lane == p, fold(front_real * rear_imag - front_imag * rear_real), acc)
        acc = jnp.where(
            place_lane == p + pings, fold(front_real * front_real + front_imag * front_imag), acc
        )
        return jnp.where(
            place_lane == p + 2 * pings, fold(rear_real * rear_real + rear_imag * rear_imag), acc
        )

    mine = correlate(0, (lead[0], lead[1]), jnp.zeros((8, 128), jnp.float32))
    mine = jnp.where((me == 0) & (place_lane < 2 * pings), 0.0, mine)
    mine = lax.fori_loop(
        1, pings, lambda p, acc: correlate(p, (row_pings[p - 1], column_pings[p - 1]), acc), mine
    )
    partial[0] = mine

    edge_forward = [
        send(rims[part].at[pl.ds(0, pings)], rims[part].at[pl.ds(3 * pings, pings)], forth)
        for part, forth in ((0, ahead), (1, above))
    ]
    edge_backward = [
        send(rims[part].at[pl.ds(0, pings)], rims[part].at[pl.ds(pings, pings)], back)
        for part, back in ((0, behind), (1, below))
    ]
    across = []
    for step in range(1, rng_size):
        across.append(
            pltpu.make_async_remote_copy(
                src_ref=partial.at[0],
                dst_ref=partial.at[step],
                send_sem=sum_send.at[owners + step],
                recv_sem=sum_recv.at[owners + step],
                device_id={"rng": (level + step) % rng_size},
                device_id_type=MESH,
            )
        )
        across[-1].start()
    for copy in across:
        copy.wait_recv()
    whole = mine
    for step in range(1, rng_size):
        whole = whole + partial[step]
    total[...] = whole
    sums[me] = whole
    spread_sums = []
    for step in range(1, owners):
        spread_sums.append(
            pltpu.make_async_remote_copy(
                src_ref=total,
                dst_ref=sums.at[me],
                send_sem=sum_send.at[step],
                recv_sem=sum_recv.at[step],
                device_id={"ping": (me + step) % owners},
                device_id_type=MESH,
            )
        )
        spread_sums[-1].start()

    relays = []
    for part, forth, back in ((0, ahead, behind), (1, above, below)):
        pool, rim = pools[part], rims[part]
        forward[part].wait_recv()
        relays.append(send(pool.at[part_of(3, 0)], pool.at[part_of(2, 0)], forth))
        backward[part].wait_recv()
        relays.append(send(pool.at[part_of(1, half)], pool.at[part_of(2, half)], back))
    for part, forth, back in ((0, ahead, behind), (1, above, below)):
        pool, rim = pools[part], rims[part]
        edge_forward[part].wait_recv()
        relays.append(send(rim.at[part_of(3, 0)], rim.at[part_of(2, 0)], forth))
        edge_backward[part].wait_recv()
        relays.append(send(rim.at[part_of(1, half)], rim.at[part_of(2, half)], back))
    for copy in spread_sums:
        copy.wait_recv()

    span = cosines.shape[1]
    along = lax.broadcasted_iota(jnp.int32, (MOST, span), 1)
    turn = turns_of(sums, list_ref[:, 0:1], list_ref[:, 1:2])
    folded = list_ref[:, 2:3] + along
    folded = jnp.where(folded >= phase_modulus, folded - phase_modulus, folded)
    square = folded * folded
    square = square - phase_modulus * (
        square.astype(jnp.float32) * (1.0 / phase_modulus)
    ).astype(jnp.int32)
    square = jnp.where(square < 0, square + phase_modulus, square)
    square = jnp.where(square >= phase_modulus, square - phase_modulus, square)
    phases = square.astype(jnp.float32) * (2.0 * math.pi / phase_modulus) + (
        list_ref[:, 3:4].astype(jnp.float32) * (math.pi / 4.0) - turn
    )
    cosines[...] = jnp.cos(phases) * scale_ref[:, 0:1]
    sines[...] = jnp.sin(phases) * scale_ref[:, 0:1]

    def spread(ref, j):
        return pltpu.roll(
            jnp.broadcast_to(ref[pl.ds(j, 1), :], (C, span)),
            span - 2 * (C - 1),
            1,
            stride=2,
            stride_axis=0,
        )[:, :X]

    def weigh(pair, carry):
        upper, lower = [], []
        for s in range(2):
            cosine = spread(cosines, 2 * pair + s)
            sine = spread(sines, 2 * pair + s)
            upper += [cosine, -sine]
            lower += [sine, cosine]
        at = pl.ds(pl.multiple_of(pair * 4 * C, 4 * C), 4 * C)
        weights[0:X, at] = jnp.concatenate(upper, axis=0).T.astype(jnp.bfloat16)
        weights[X : 2 * X, at] = jnp.concatenate(lower, axis=0).T.astype(jnp.bfloat16)
        return carry

    lax.fori_loop(0, MOST // 2, weigh, 0)

    for copy in forward[2:] + backward[2:] + relays:
        copy.wait_recv()

    targets = []
    for k in range(1, HOLD):
        for part in range(2):
            d, dc = k // CORES, k % CORES
            to = device(y + d, x, c + dc) if part == 0 else device(y, x + d, c + dc)
            targets.append((part * HOLD + k, to))
    tiles = length // 128

    def cut(q, part, slot):
        local = table[0, part * HOLD * HOLD + slot]
        offset = table[1, part * HOLD * HOLD + slot]
        pool = pools[part]
        back = offset < 0
        rem = jnp.where(back, offset + 128, offset)
        turn = lax.rem(128 - rem, 128)
        keep = lane < 128 - rem
        first = q * wide // 128

        def tile(k):
            if k < 0 or k >= tiles:
                return rims[part][local].astype(jnp.float32)
            return pool[local, :, 128 * k : 128 * (k + 1)].astype(jnp.float32)

        here = tile(first)
        current = pltpu.roll(jnp.where(back, tile(first - 1), here), turn, 1)
        out = []
        for k in range(first, first + wide // 128):
            following_tile = tile(k + 1)
            following = pltpu.roll(jnp.where(back, here, following_tile), turn, 1)
            out.append(jnp.where(keep, current, following).astype(jnp.bfloat16))
            current, here = following, following_tile
        return out

    def build(q):
        for part in range(2):

            def for_self(s, carry):
                for k, value in enumerate(cut(q, part, s)):
                    received[q][part * HOLD * HOLD + s, :, 128 * k : 128 * (k + 1)] = value
                return carry

            def for_others(s, carry):
                for k, value in enumerate(cut(q, part, s)):
                    staging[q % 2, part * HOLD * HOLD + s, :, 128 * k : 128 * (k + 1)] = value
                return carry

            lax.fori_loop(0, HOLD, for_self, 0)
            lax.fori_loop(HOLD, HOLD * HOLD, for_others, 0)

    def ship(q):
        copies = []
        for i, (group, to) in enumerate(targets):
            at = pl.ds(group * HOLD, HOLD)
            copies.append(
                pltpu.make_async_remote_copy(
                    src_ref=staging.at[q % 2, at],
                    dst_ref=received[q].at[at],
                    send_sem=slot_send.at[q, i],
                    recv_sem=slot_recv.at[q, i],
                    device_id={"ping": to},
                    device_id_type=MESH,
                )
            )
            copies[-1].start()
        return copies

    shipped = []
    for q in range(2):
        build(q)
        shipped.append(ship(q))
    rows = X
    for q in range(chunks):
        if q + 2 < chunks:
            for copy in shipped[q]:
                copy.wait_send()
            build(q + 2)
            shipped.append(ship(q + 2))
        for copy in shipped[q]:
            copy.wait_recv()

        def fill(j, carry):
            for part in range(2):
                at = pl.multiple_of(j * 2 * C + part * C, C)
                stacked[pl.ds(at, C), :] = received[q][arrival[part, j]]
            return carry

        lax.fori_loop(0, MOST, fill, 0)
        before[q].wait()

        def multiply(i, carry):
            at = pl.ds(pl.multiple_of(i * rows, rows), rows)
            product = jnp.dot(weights[at, :], stacked[...], preferred_element_type=jnp.float32)
            image[q % 2, at, :] = (image[q % 2, at, :].astype(jnp.float32) + product).astype(
                jnp.bfloat16
            )
            return carry

        lax.fori_loop(0, 2 * X // rows, multiply, 0)
        after[q].start()
        if q >= 1 and q + 1 < chunks:
            after[q - 1].wait()
            before[q + 1].start()
    for copy in started + across + spread_sums + shipped[chunks - 2] + shipped[chunks - 1]:
        copy.wait_send()
    for copy in after[chunks - 2 :]:
        copy.wait()


def focus(table, arrival, echoes, front_pick, rear_pick, entries, scales, earlier, rng_size):
    pings, parts, channels, length = echoes.shape
    owners = SIDE * SIDE * CORES
    chunks = 8
    wide = length // chunks
    slots = 2 * HOLD * HOLD
    count = 2 * (HOLD - 1)
    bf16, f32 = jnp.bfloat16, jnp.float32
    dma = pltpu.SemaphoreType.DMA
    steps = 3 + 8 + 4 + 8
    smem = pl.BlockSpec(memory_space=pltpu.SMEM)
    return pl.pallas_call(
        functools.partial(image_kernel, rng_size),
        out_shape=jax.ShapeDtypeStruct((2 * X, length), bf16),
        in_specs=[smem, smem, ANY, IN_VMEM, IN_VMEM, IN_VMEM, IN_VMEM, ANY],
        out_specs=ANY,
        scratch_shapes=[
            pltpu.VMEM((SIDE * pings, channels, length), bf16),
            pltpu.VMEM((SIDE * pings, channels, length), bf16),
            pltpu.VMEM((SIDE * pings, channels, 128), bf16),
            pltpu.VMEM((SIDE * pings, channels, 128), bf16),
            pltpu.VMEM((parts, channels, length), bf16),
            pltpu.VMEM((2, pings, parts, channels, 128), bf16),
            pltpu.VMEM((rng_size, 8, 128), f32),
            pltpu.VMEM((8, 128), f32),
            pltpu.VMEM((owners, 8, 128), f32),
            pltpu.VMEM((2, slots, channels, wide), bf16),
            pltpu.VMEM((2 * X, MOST * 2 * C), bf16),
            pltpu.VMEM((MOST * 2 * C, wide), bf16),
            pltpu.VMEM((2, 2 * X, wide), bf16),
            pltpu.VMEM((MOST, X + 128), f32),
            pltpu.VMEM((MOST, X + 128), f32),
            dma((2 + 2 * chunks,)),
            dma((steps,)),
            dma((steps,)),
            dma((owners + rng_size,)),
            dma((owners + rng_size,)),
            dma((chunks, count)),
            dma((chunks, count)),
        ]
        + [pltpu.VMEM((slots, channels, wide), bf16)] * chunks,
        compiler_params=pltpu.CompilerParams(
            collective_id=0, has_side_effects=True, vmem_limit_bytes=63 << 20
        ),
        name="focus",
    )(table, arrival, echoes, front_pick, rear_pick, entries, scales, earlier)


def rank_in(groups, positions):
    same = (groups[:, None, :] == groups[:, :, None]) & (positions[None, :] < positions[:, None])[None]
    return jnp.sum(same.astype(jnp.int32), axis=2)


def per_device(echoes, pairing, footprint, counts, offsets, earlier):
    block_len = echoes.shape[3]
    owners = lax.axis_size("ping")
    rng_size = lax.axis_size("rng")
    me = lax.axis_index("ping")
    y, x, c = place(me)

    channel_ids = jnp.arange(C, dtype=jnp.int32)
    front_pick = (pairing[:, 0, :, None] == channel_ids).astype(jnp.bfloat16)
    rear_pick = (pairing[:, 1, :, None] == channel_ids).astype(jnp.bfloat16)

    steps = jnp.arange(HOLD, dtype=jnp.int32)
    tiles = jnp.concatenate(
        [
            device(y + steps // CORES, x, c + steps % CORES),
            device(y, x + steps // CORES, c + steps % CORES),
        ]
    )
    all_tiles = jnp.arange(owners, dtype=jnp.int32)
    chosen = (tiles[:, None] == all_tiles[None, :]).astype(jnp.int32)
    positions = jnp.arange(MOST, dtype=jnp.int32)
    foot = jnp.sum(chosen[:, :, None] * footprint[None], axis=1)
    shift = jnp.sum(chosen[:, :, None] * offsets[None], axis=1)
    count = jnp.sum(chosen * counts[None, :], axis=1)
    listed = positions[None, :] < count[:, None]
    oy, ox, oc = place(foot // PING_DEV)
    by_row = steps[:, None] >= 0
    by_row = jnp.concatenate([by_row, ~by_row], axis=0)
    group = jnp.where(listed, jnp.where(by_row, oy, ox) * CORES + oc, -1)
    rank = rank_in(group, positions)
    here = group == jnp.where(by_row, y, x) * CORES + c
    distance = jnp.where(by_row, ox - x + SIDE, oy - y + SIDE) % SIDE
    source = distance * PING_DEV + foot % PING_DEV
    fits = (here[:, None, :] & (rank[:, None, :] == steps[None, :, None])).astype(jnp.int32)
    table = jnp.stack(
        [
            jnp.sum(fits * source[:, None, :], axis=2).reshape(-1),
            jnp.sum(fits * shift[:, None, :], axis=2).reshape(-1),
        ]
    )
    own_group = jnp.stack([group[0], group[HOLD]])
    own_rank = jnp.stack([rank[0], rank[HOLD]])
    own_place = jnp.stack([y, x])[:, None]
    own_distance = (own_place - own_group // CORES + SIDE) % SIDE
    own_core = (c - own_group % CORES + CORES) % CORES
    arrival = (own_distance * CORES + own_core) * HOLD + own_rank
    arrival = jnp.where(listed[0:1], arrival, arrival[:, 0:1])
    arrival = arrival + jnp.array([[0], [HOLD * HOLD]], jnp.int32)
    entries = jnp.stack(
        [
            foot[0] // PING_DEV,
            foot[0] % PING_DEV,
            jnp.remainder(me * X - foot[0] * SPACING - 2 * (C - 1), phase_modulus),
            shift[0],
        ],
        axis=1,
    )
    scales = listed[0].astype(jnp.float32) / jnp.sqrt(jnp.float32(C) * count[0].astype(jnp.float32))
    image = focus(
        table,
        arrival,
        echoes,
        front_pick,
        rear_pick,
        entries,
        scales[:, None],
        earlier.reshape(2 * X, block_len),
        rng_size,
    )
    return image.reshape(earlier.shape)


def solution(mesh):
    return jax.shard_map(
        per_device,
        mesh=mesh,
        in_specs=(
            P("ping", None, None, "rng"),
            P("ping", None, None),
            P(),
            P(),
            P(),
            P("ping", None, None, "rng"),
        ),
        out_specs=P("ping", None, None, "rng"),
        check_vma=False,
    )
```

time: 682 us -> 231 us (0.34); the launches traced: 670 us -> 230 us
  local copies, waits for them, and re-layouts: 273 us -> 11 us
  Pallas kernels: 0 us -> 214 us
  waiting for transfers between devices: 126 us -> 0 us
  other arithmetic: 101 us -> 5.32 us
  blocking collectives: 77.3 us -> 0 us
  matrix products: 51.7 us -> 0 us
  loops' own time: 21.6 us -> 0 us
  starting transfers between devices: 18.2 us -> 0 us
    gather x192 -> x0, local copies, waits for them, and re-layouts: 238 us -> none
    pallas_call x0 -> x1, Pallas kernels: none -> 214 us  [focus(): pl.pallas_call(functools.partial(image_kernel, rng_size), out_shape=jax.S...]
    all_to_all x2 -> x0, waiting for transfers between devices: 121 us -> none  [the longest x1 121 us: per_device(): lax.all_to_all(outgoing, 'ping', split_axis=0, concat_axis=0, tiled=True)]
    another operation x6 -> x3, other arithmetic: 88 us -> 0.67 us  [the longest x1 0.58 us: per_device(): jnp.stack([jnp.sum(fits * source[:, None, :], axis=2).reshape(-1), jnp.su...]
    all_gather x1 -> x0, blocking collectives: 65.6 us -> none  [prefix(): everything = lax.all_gather(shard, axis)]
    dot_general x4 -> x0, matrix products: 51.7 us -> none  [the longest x1 44.6 us: focus_tile(): jnp.dot(weights, flat_rows.reshape(-1, block_len), preferred_element_type...]
    another operation x2 -> x0, loops' own time: 21.6 us -> none  [the longest x1 21.5 us: prefix(): return lax.fori_loop(0, length, step, start)]
    dynamic_slice x32 -> x0, local copies, waits for them, and re-layouts: 18.8 us -> none  [step(): new = combine(before, everything[k])]
  transfers between devices with their start and end apart: 5 -> 0, of which waited for: 3 -> 0; matrix products, arithmetic and copies ran while one was open for 57% -> 0% of each run, Pallas kernels for 0% -> 0%
where the time goes in v4:
time: 231 us; the launch traced here: 230 us
  Pallas kernels  214 us (93%)
  local copies, waits for them, and re-layouts  11 us (5%)
  other arithmetic  5.32 us (2%)
    pallas_call x1, Pallas kernels, focus(): pl.pallas_call(functools.partial(image_kernel, rng_size), out_shape=jax.S...  214 us
    unnamed x1, local copies, waits for them, and re-layouts  8.44 us

profile of v4, /device:TPU:0, one launch (start us, length us, event | category | flops | bytes accessed | tf_op | source)
XLA Modules:
  0.0 230.2 jit_solution(15637250291013031670)
XLA Ops:
  0.0 0.1 pad_add_fusion.3
  0.1 0.8 select_reduce_fusion.2
  1.0 0.1 pad_add_fusion.4
  1.2 0.1 fusion.10
  1.2 0.9 multiply_reduce_fusion.1
  2.2 0.1 fusion.9
  2.3 0.1 broadcast_compare_fusion
  2.4 0.5 convert_reduce_fusion
  2.9 0.6 select_reduce_fusion.1
  3.5 0.1 stack_reshape.6
  3.6 0.1 stack_reshape.7
  3.7 0.6 pad_add_fusion.1.table
  4.3 0.1 add_add_fusion
  4.4 0.1 slice_reduce_fusion
  4.5 0.6 select_add_fusion.arrival
  5.1 0.7 slice_bitcast_fusion
  5.8 0.1 copy.31
  5.9 0.1 copy.30
  6.0 0.7 copy.32.list_ref
  6.7 0.7 copy.33.scale_ref
  7.3 0.7 fusion.1
  8.1 213.7 %focus.1 = bf16[2048,2048]{1,0:T(8,128)(2,1)} custom-call(s32[2,128]{1,0:T(2,128)} %pad_add_fusion.1.table, s32[2,48]{1,0:T(2,128)} %select_add_fusion.arrival, bf16[16,2,32,2048]{3,2,1,0:T(8,128)(2,1)} %echo_ref.1, bf16[16,8,32]{2,1,0:T(8,128)(2,1)} %get-tuple-element.23.front_ref, bf16[16,8,32]{2,1,0:T(8,128)(2,1)} %get-tuple-element.24.rear_ref, ...), custom_call_target="tpu_custom_call" | custom-call | tf_op jit(solution)/shard_map/focus/pallas_call | solution.py:457
  221.7 8.4 %copy.35 = bf16[1,2,1024,2048]{3,2,1,0:T(8,128)(2,1)} copy(bf16[1,2,1024,2048]{3,2,1,0:T(8,128)(2,1)} %bitcast.25) | data formatting | bytes 16777216
  (14 shorter events, 0.1 us)

commit v5 on v4

--- a/solution.py
+++ b/solution.py
@@ -381,8 +381,8 @@
                     staging[q % 2, part * HOLD * HOLD + s, :, 128 * k : 128 * (k + 1)] = value
                 return carry
 
-            lax.fori_loop(0, HOLD, for_self, 0)
-            lax.fori_loop(HOLD, HOLD * HOLD, for_others, 0)
+            lax.fori_loop(0, HOLD, for_self, 0, unroll=True)
+            lax.fori_loop(HOLD, HOLD * HOLD, for_others, 0, unroll=HOLD)
 
     def ship(q):
         copies = []
@@ -421,7 +421,7 @@
                 stacked[pl.ds(at, C), :] = received[q][arrival[part, j]]
             return carry
 
-        lax.fori_loop(0, MOST, fill, 0)
+        lax.fori_loop(0, MOST, fill, 0, unroll=8)
         before[q].wait()
 
         def multiply(i, carry):

time: 231 us -> 206 us (0.89)
  Pallas kernels: 214 us -> 188 us
    pallas_call x1, Pallas kernels: 214 us -> 188 us  [focus(): pl.pallas_call(functools.partial(image_kernel, rng_size), out_shape=jax.S...]
where the time goes in v5:
time: 206 us; the launch traced here: 205 us
  Pallas kernels  188 us (91%)
  local copies, waits for them, and re-layouts  11 us (5%)
  other arithmetic  5.32 us (3%)
    pallas_call x1, Pallas kernels, focus(): pl.pallas_call(functools.partial(image_kernel, rng_size), out_shape=jax.S...  188 us
    unnamed x1, local copies, waits for them, and re-layouts  8.44 us

profile of v5, /device:TPU:0, one launch (start us, length us, event | category | flops | bytes accessed | tf_op | source)
XLA Modules:
  0.0 205.0 jit_solution(7737778210429313553)
XLA Ops:
  0.0 0.1 pad_add_fusion.3
  0.1 0.8 select_reduce_fusion.2
  1.0 0.1 pad_add_fusion.4
  1.2 0.1 fusion.10
  1.2 0.9 multiply_reduce_fusion.1
  2.2 0.1 fusion.9
  2.3 0.1 broadcast_compare_fusion
  2.4 0.5 convert_reduce_fusion
  2.9 0.6 select_reduce_fusion.1
  3.5 0.1 stack_reshape.6
  3.6 0.1 stack_reshape.7
  3.7 0.6 pad_add_fusion.1.table
  4.3 0.1 add_add_fusion
  4.4 0.1 slice_reduce_fusion
  4.5 0.6 select_add_fusion.arrival
  5.1 0.7 slice_bitcast_fusion
  5.8 0.1 copy.31
  5.9 0.1 copy.30
  6.0 0.7 copy.32.list_ref
  6.7 0.7 copy.33.scale_ref
  7.3 0.7 fusion.1
  8.1 188.5 %focus.1 = bf16[2048,2048]{1,0:T(8,128)(2,1)} custom-call(s32[2,128]{1,0:T(2,128)} %pad_add_fusion.1.table, s32[2,48]{1,0:T(2,128)} %select_add_fusion.arrival, bf16[16,2,32,2048]{3,2,1,0:T(8,128)(2,1)} %echo_ref.1, bf16[16,8,32]{2,1,0:T(8,128)(2,1)} %get-tuple-element.23.front_ref, bf16[16,8,32]{2,1,0:T(8,128)(2,1)} %get-tuple-element.24.rear_ref, ...), custom_call_target="tpu_custom_call" | custom-call | tf_op jit(solution)/shard_map/focus/pallas_call | solution.py:457
  196.6 8.4 %copy.35 = bf16[1,2,1024,2048]{3,2,1,0:T(8,128)(2,1)} copy(bf16[1,2,1024,2048]{3,2,1,0:T(8,128)(2,1)} %bitcast.25) | data formatting | bytes 16777216
  (14 shorter events, 0.1 us)

commit v6 on v5

--- a/solution.py
+++ b/solution.py
@@ -74,12 +74,15 @@
     scale_ref,
     earlier_ref,
     out_ref,
-    row_pings,
-    column_pings,
-    row_edges,
-    column_edges,
+    row_first,
+    row_second,
+    column_first,
+    column_second,
+    row_low,
+    row_high,
+    column_low,
+    column_high,
     lead,
-    beside,
     partial,
     total,
     sums,
@@ -96,6 +99,8 @@
     sum_recv,
     slot_send,
     slot_recv,
+    edge_send,
+    edge_recv,
     *received,
 ):
     me = lax.axis_index("ping")
@@ -105,6 +110,7 @@
     pings, half = PING_DEV, PING_DEV // 2
     length = echo_ref.shape[3]
     chunks, wide = len(received), stacked.shape[1]
+    order = [1, 2, 4, 5, 6, 3, 0, 7]
 
     barrier = pltpu.get_barrier_semaphore()
     for step in range(1, owners):
@@ -115,19 +121,28 @@
         pl.semaphore_signal(
             barrier, inc=1, device_id={"rng": (level + step) % rng_size}, device_id_type=MESH
         )
+    pools = ((row_first, row_second), (column_first, column_second))
+    lows, highs = (row_low, column_low), (row_high, column_high)
+    span = length // 2
+    spans = (pl.ds(0, span), pl.ds(span, span))
     own = [
-        pltpu.make_async_copy(echo_ref.at[:, 0], row_pings.at[pl.ds(0, pings)], local_sem.at[0]),
-        pltpu.make_async_copy(echo_ref.at[:, 1], column_pings.at[pl.ds(0, pings)], local_sem.at[1]),
+        pltpu.make_async_copy(
+            echo_ref.at[:, part, :, spans[h]],
+            pools[part][h].at[pl.ds(0, pings)],
+            local_sem.at[2 * chunks + 2 * part + h],
+        )
+        for part in range(2)
+        for h in range(2)
     ]
     before = [
         pltpu.make_async_copy(
-            earlier_ref.at[:, pl.ds(q * wide, wide)], image.at[q % 2], local_sem.at[2 + q]
+            earlier_ref.at[:, pl.ds(order[q] * wide, wide)], image.at[q % 2], local_sem.at[q]
         )
         for q in range(chunks)
     ]
     after = [
         pltpu.make_async_copy(
-            image.at[q % 2], out_ref.at[:, pl.ds(q * wide, wide)], local_sem.at[2 + chunks + q]
+            image.at[q % 2], out_ref.at[:, pl.ds(order[q] * wide, wide)], local_sem.at[chunks + q]
         )
         for q in range(chunks)
     ]
@@ -162,52 +177,73 @@
         return pl.ds(distance * pings + start, half)
 
     from_lead = send(echo_ref.at[pings - 1], lead, {"ping": (me + 1) % owners})
-    from_low = send(echo_ref.at[:, :, :, pl.ds(length - 128, 128)], beside.at[0], up)
-    from_high = send(echo_ref.at[:, :, :, pl.ds(0, 128)], beside.at[1], down)
-    forward, backward = [], []
-    for turn in range(2):
-        for part, pool, forth, back in (
-            (0, row_pings, ahead, behind),
-            (1, column_pings, above, below),
-        ):
-            first, second = (low, high) if turn == 0 else (high, low)
-            forward.append(
-                send(echo_ref.at[first, part], pool.at[part_of(3, turn * half)], forth)
-            )
-            backward.append(
-                send(echo_ref.at[second, part], pool.at[part_of(1, (1 - turn) * half)], back)
-            )
-
-    from_low.wait_recv()
-    from_high.wait_recv()
+
+    edge_copies = []
+
+    def send_edges(sources_low, sources_high, at):
+        for part in range(2):
+            for source, pool, target in (
+                (sources_low[part], lows[part], up),
+                (sources_high[part], highs[part], down),
+            ):
+                i = len(edge_copies)
+                edge_copies.append(
+                    pltpu.make_async_remote_copy(
+                        src_ref=source,
+                        dst_ref=pool.at[at],
+                        send_sem=edge_send.at[i],
+                        recv_sem=edge_recv.at[i],
+                        device_id=target,
+                        device_id_type=MESH,
+                    )
+                )
+                edge_copies[-1].start()
+
+    def send_gathered_edges(distance):
+        at = pl.ds(distance * pings, pings)
+        send_edges(
+            [pools[part][1].at[at, :, pl.ds(span - 128, 128)] for part in range(2)],
+            [pools[part][0].at[at, :, pl.ds(0, 128)] for part in range(2)],
+            at,
+        )
+
+    send_edges(
+        [echo_ref.at[:, part, :, pl.ds(length - 128, 128)] for part in range(2)],
+        [echo_ref.at[:, part, :, pl.ds(0, 128)] for part in range(2)],
+        pl.ds(0, pings),
+    )
+    ways = ((0, ahead, behind), (1, above, below))
+    forward, backward = [[], []], [[], []]
+    for h in range(2):
+        for turn in range(2):
+            for part, forth, back in ways:
+                first, second = (low, high) if turn == 0 else (high, low)
+                pool = pools[part][h]
+                forward[h].append(
+                    send(
+                        echo_ref.at[first, part, :, spans[h]], pool.at[part_of(3, turn * half)], forth
+                    )
+                )
+                backward[h].append(
+                    send(
+                        echo_ref.at[second, part, :, spans[h]],
+                        pool.at[part_of(1, (1 - turn) * half)],
+                        back,
+                    )
+                )
+
     lane = lax.broadcasted_iota(jnp.int32, (C, 128), 1)
     use_low = level > 0
     use_high = level < rng_size - 1
-    pools = (row_pings, column_pings)
-    rims = (row_edges, column_edges)
-
-    def merge(p, carry):
-        for part in range(2):
-            low_edge = beside[0, p, part].astype(jnp.float32)
-            high_edge = beside[1, p, part].astype(jnp.float32)
-            merged = jnp.where(
-                lane < 64,
-                jnp.where(use_high, high_edge, 0.0),
-                jnp.where(use_low, low_edge, 0.0),
-            )
-            rims[part][p] = merged.astype(jnp.bfloat16)
-        return carry
-
-    lax.fori_loop(0, pings, merge, 0)
 
     for copy in own:
         copy.wait()
     from_lead.wait_recv()
-    place_lane = lax.broadcasted_iota(jnp.int32, (8, 128), 1)
+    place_lane = lax.broadcasted_iota(jnp.int32, (1, 128), 1)
 
     def fold(value):
         out = value[:, 0:128]
-        for k in range(1, length // 128):
+        for k in range(1, span // 128):
             out = out + value[:, 128 * k : 128 * (k + 1)]
         out = jnp.sum(out, axis=0, keepdims=True)
         return jnp.sum(out, axis=1, keepdims=True)
@@ -215,33 +251,28 @@
     def correlate(p, front_source, acc):
         front, rear = front_ref[p], rear_ref[p]
         dot = functools.partial(jnp.dot, preferred_element_type=jnp.float32)
-        front_real = dot(front, front_source[0])
-        front_imag = dot(front, front_source[1])
-        rear_real = dot(rear, row_pings[p])
-        rear_imag = dot(rear, column_pings[p])
-        acc = jnp.where(place_lane == p, fold(front_real * rear_imag - front_imag * rear_real), acc)
-        acc = jnp.where(
-            place_lane == p + pings, fold(front_real * front_real + front_imag * front_imag), acc
-        )
-        return jnp.where(
-            place_lane == p + 2 * pings, fold(rear_real * rear_real + rear_imag * rear_imag), acc
-        )
-
-    mine = correlate(0, (lead[0], lead[1]), jnp.zeros((8, 128), jnp.float32))
+        cross = front_energy = rear_energy = 0.0
+        for h in range(2):
+            front_real = dot(front, front_source(0, h))
+            front_imag = dot(front, front_source(1, h))
+            rear_real = dot(rear, pools[0][h][p])
+            rear_imag = dot(rear, pools[1][h][p])
+            cross = cross + fold(front_real * rear_imag - front_imag * rear_real)
+            front_energy = front_energy + fold(front_real * front_real + front_imag * front_imag)
+            rear_energy = rear_energy + fold(rear_real * rear_real + rear_imag * rear_imag)
+        acc = jnp.where(place_lane == p, cross, acc)
+        acc = jnp.where(place_lane == p + pings, front_energy, acc)
+        return jnp.where(place_lane == p + 2 * pings, rear_energy, acc)
+
+    mine = correlate(
+        0, lambda part, h: lead[part, :, span * h : span * (h + 1)], jnp.zeros((1, 128), jnp.float32)
+    )
     mine = jnp.where((me == 0) & (place_lane < 2 * pings), 0.0, mine)
     mine = lax.fori_loop(
-        1, pings, lambda p, acc: correlate(p, (row_pings[p - 1], column_pings[p - 1]), acc), mine
+        1, pings, lambda p, acc: correlate(p, lambda part, h: pools[part][h][p - 1], acc), mine
     )
     partial[0] = mine
 
-    edge_forward = [
-        send(rims[part].at[pl.ds(0, pings)], rims[part].at[pl.ds(3 * pings, pings)], forth)
-        for part, forth in ((0, ahead), (1, above))
-    ]
-    edge_backward = [
-        send(rims[part].at[pl.ds(0, pings)], rims[part].at[pl.ds(pings, pings)], back)
-        for part, back in ((0, behind), (1, below))
-    ]
     across = []
     for step in range(1, rng_size):
         across.append(
@@ -276,24 +307,19 @@
         )
         spread_sums[-1].start()
 
-    relays = []
-    for part, forth, back in ((0, ahead, behind), (1, above, below)):
-        pool, rim = pools[part], rims[part]
-        forward[part].wait_recv()
-        relays.append(send(pool.at[part_of(3, 0)], pool.at[part_of(2, 0)], forth))
-        backward[part].wait_recv()
-        relays.append(send(pool.at[part_of(1, half)], pool.at[part_of(2, half)], back))
-    for part, forth, back in ((0, ahead, behind), (1, above, below)):
-        pool, rim = pools[part], rims[part]
-        edge_forward[part].wait_recv()
-        relays.append(send(rim.at[part_of(3, 0)], rim.at[part_of(2, 0)], forth))
-        edge_backward[part].wait_recv()
-        relays.append(send(rim.at[part_of(1, half)], rim.at[part_of(2, half)], back))
+    relays = [[], []]
+    for h in range(2):
+        for part, forth, back in ways:
+            pool = pools[part][h]
+            forward[h][part].wait_recv()
+            relays[h].append(send(pool.at[part_of(3, 0)], pool.at[part_of(2, 0)], forth))
+            backward[h][part].wait_recv()
+            relays[h].append(send(pool.at[part_of(1, half)], pool.at[part_of(2, half)], back))
     for copy in spread_sums:
         copy.wait_recv()
 
-    span = cosines.shape[1]
-    along = lax.broadcasted_iota(jnp.int32, (MOST, span), 1)
+    chirp = cosines.shape[1]
+    along = lax.broadcasted_iota(jnp.int32, (MOST, chirp), 1)
     turn = turns_of(sums, list_ref[:, 0:1], list_ref[:, 1:2])
     folded = list_ref[:, 2:3] + along
     folded = jnp.where(folded >= phase_modulus, folded - phase_modulus, folded)
@@ -311,8 +337,8 @@
 
     def spread(ref, j):
         return pltpu.roll(
-            jnp.broadcast_to(ref[pl.ds(j, 1), :], (C, span)),
-            span - 2 * (C - 1),
+            jnp.broadcast_to(ref[pl.ds(j, 1), :], (C, chirp)),
+            chirp - 2 * (C - 1),
             1,
             stride=2,
             stride_axis=0,
@@ -332,7 +358,7 @@
 
     lax.fori_loop(0, MOST // 2, weigh, 0)
 
-    for copy in forward[2:] + backward[2:] + relays:
+    for copy in forward[0][2:] + backward[0][2:] + relays[0]:
         copy.wait_recv()
 
     targets = []
@@ -346,7 +372,6 @@
     def cut(q, part, slot):
         local = table[0, part * HOLD * HOLD + slot]
         offset = table[1, part * HOLD * HOLD + slot]
-        pool = pools[part]
         back = offset < 0
         rem = jnp.where(back, offset + 128, offset)
         turn = lax.rem(128 - rem, 128)
@@ -354,9 +379,12 @@
         first = q * wide // 128
 
         def tile(k):
-            if k < 0 or k >= tiles:
-                return rims[part][local].astype(jnp.float32)
-            return pool[local, :, 128 * k : 128 * (k + 1)].astype(jnp.float32)
+            if k < 0:
+                return jnp.where(use_low, lows[part][local].astype(jnp.float32), 0.0)
+            if k >= tiles:
+                return jnp.where(use_high, highs[part][local].astype(jnp.float32), 0.0)
+            at = 128 * k % span
+            return pools[part][128 * k // span][local, :, at : at + 128].astype(jnp.float32)
 
         here = tile(first)
         current = pltpu.roll(jnp.where(back, tile(first - 1), here), turn, 1)
@@ -368,32 +396,33 @@
             current, here = following, following_tile
         return out
 
-    def build(q):
+    def build(i):
+        q = order[i]
         for part in range(2):
 
             def for_self(s, carry):
                 for k, value in enumerate(cut(q, part, s)):
-                    received[q][part * HOLD * HOLD + s, :, 128 * k : 128 * (k + 1)] = value
+                    received[i][part * HOLD * HOLD + s, :, 128 * k : 128 * (k + 1)] = value
                 return carry
 
             def for_others(s, carry):
                 for k, value in enumerate(cut(q, part, s)):
-                    staging[q % 2, part * HOLD * HOLD + s, :, 128 * k : 128 * (k + 1)] = value
+                    staging[i % 2, part * HOLD * HOLD + s, :, 128 * k : 128 * (k + 1)] = value
                 return carry
 
             lax.fori_loop(0, HOLD, for_self, 0, unroll=True)
             lax.fori_loop(HOLD, HOLD * HOLD, for_others, 0, unroll=HOLD)
 
-    def ship(q):
+    def ship(i):
         copies = []
-        for i, (group, to) in enumerate(targets):
+        for k, (group, to) in enumerate(targets):
             at = pl.ds(group * HOLD, HOLD)
             copies.append(
                 pltpu.make_async_remote_copy(
-                    src_ref=staging.at[q % 2, at],
-                    dst_ref=received[q].at[at],
-                    send_sem=slot_send.at[q, i],
-                    recv_sem=slot_recv.at[q, i],
+                    src_ref=staging.at[i % 2, at],
+                    dst_ref=received[i].at[at],
+                    send_sem=slot_send.at[i, k],
+                    recv_sem=slot_recv.at[i, k],
                     device_id={"ping": to},
                     device_id_type=MESH,
                 )
@@ -402,42 +431,49 @@
         return copies
 
     shipped = []
-    for q in range(2):
-        build(q)
-        shipped.append(ship(q))
+    for i in range(2):
+        build(i)
+        shipped.append(ship(i))
+    for copy in forward[1][2:] + backward[1][2:] + relays[1]:
+        copy.wait_recv()
+    for distance in range(1, SIDE):
+        send_gathered_edges(distance)
     rows = X
-    for q in range(chunks):
-        if q + 2 < chunks:
-            for copy in shipped[q]:
+    for i in range(chunks):
+        if i + 2 < chunks:
+            for copy in shipped[i]:
                 copy.wait_send()
-            build(q + 2)
-            shipped.append(ship(q + 2))
-        for copy in shipped[q]:
+            if i + 2 == order.index(0):
+                for copy in edge_copies:
+                    copy.wait_recv()
+            build(i + 2)
+            shipped.append(ship(i + 2))
+        for copy in shipped[i]:
             copy.wait_recv()
 
         def fill(j, carry):
             for part in range(2):
                 at = pl.multiple_of(j * 2 * C + part * C, C)
-                stacked[pl.ds(at, C), :] = received[q][arrival[part, j]]
+                stacked[pl.ds(at, C), :] = received[i][arrival[part, j]]
             return carry
 
         lax.fori_loop(0, MOST, fill, 0, unroll=8)
-        before[q].wait()
-
-        def multiply(i, carry):
-            at = pl.ds(pl.multiple_of(i * rows, rows), rows)
+        before[i].wait()
+
+        def multiply(k, carry):
+            at = pl.ds(pl.multiple_of(k * rows, rows), rows)
             product = jnp.dot(weights[at, :], stacked[...], preferred_element_type=jnp.float32)
-            image[q % 2, at, :] = (image[q % 2, at, :].astype(jnp.float32) + product).astype(
+            image[i % 2, at, :] = (image[i % 2, at, :].astype(jnp.float32) + product).astype(
                 jnp.bfloat16
             )
             return carry
 
         lax.fori_loop(0, 2 * X // rows, multiply, 0)
-        after[q].start()
-        if q >= 1 and q + 1 < chunks:
-            after[q - 1].wait()
-            before[q + 1].start()
-    for copy in started + across + spread_sums + shipped[chunks - 2] + shipped[chunks - 1]:
+        after[i].start()
+        if i >= 1 and i + 1 < chunks:
+            after[i - 1].wait()
+            before[i + 1].start()
+    for copy in started + across + edge_copies + spread_sums + shipped[chunks - 2] + shipped[chunks - 1]:
         copy.wait_send()
     for copy in after[chunks - 2 :]:
         copy.wait()
@@ -452,7 +488,7 @@
     count = 2 * (HOLD - 1)
     bf16, f32 = jnp.bfloat16, jnp.float32
     dma = pltpu.SemaphoreType.DMA
-    steps = 3 + 8 + 4 + 8
+    steps = 1 + 16 + 8
     smem = pl.BlockSpec(memory_space=pltpu.SMEM)
     return pl.pallas_call(
         functools.partial(image_kernel, rng_size),
@@ -460,28 +496,27 @@
         in_specs=[smem, smem, ANY, IN_VMEM, IN_VMEM, IN_VMEM, IN_VMEM, ANY],
         out_specs=ANY,
         scratch_shapes=[
-            pltpu.VMEM((SIDE * pings, channels, length), bf16),
-            pltpu.VMEM((SIDE * pings, channels, length), bf16),
-            pltpu.VMEM((SIDE * pings, channels, 128), bf16),
-            pltpu.VMEM((SIDE * pings, channels, 128), bf16),
+            *[pltpu.VMEM((SIDE * pings, channels, length // 2), bf16)] * 4,
+            *[pltpu.VMEM((SIDE * pings, channels, 128), bf16)] * 4,
             pltpu.VMEM((parts, channels, length), bf16),
-            pltpu.VMEM((2, pings, parts, channels, 128), bf16),
-            pltpu.VMEM((rng_size, 8, 128), f32),
-            pltpu.VMEM((8, 128), f32),
-            pltpu.VMEM((owners, 8, 128), f32),
+            pltpu.VMEM((rng_size, 1, 128), f32),
+            pltpu.VMEM((1, 128), f32),
+            pltpu.VMEM((owners, 1, 128), f32),
             pltpu.VMEM((2, slots, channels, wide), bf16),
             pltpu.VMEM((2 * X, MOST * 2 * C), bf16),
             pltpu.VMEM((MOST * 2 * C, wide), bf16),
             pltpu.VMEM((2, 2 * X, wide), bf16),
             pltpu.VMEM((MOST, X + 128), f32),
             pltpu.VMEM((MOST, X + 128), f32),
-            dma((2 + 2 * chunks,)),
+            dma((4 + 2 * chunks,)),
             dma((steps,)),
             dma((steps,)),
             dma((owners + rng_size,)),
             dma((owners + rng_size,)),
             dma((chunks, count)),
             dma((chunks, count)),
+            dma((4 * SIDE,)),
+            dma((4 * SIDE,)),
         ]
         + [pltpu.VMEM((slots, channels, wide), bf16)] * chunks,
         compiler_params=pltpu.CompilerParams(
@@ -489,6 +524,37 @@
         ),
         name="focus",
     )(table, arrival, echoes, front_pick, rear_pick, entries, scales, earlier)
+
+
+def move_kernel(source, target, held, load_sem, store_sem):
+    pieces = load_sem.shape[0]
+    rows = held.shape[0] // pieces
+    loads, stores = [], []
+    for i in range(pieces):
+        at = pl.ds(rows * i, rows)
+        loads.append(pltpu.make_async_copy(source.at[at], held.at[at], load_sem.at[i]))
+        stores.append(pltpu.make_async_copy(held.at[at], target.at[at], store_sem.at[i]))
+        loads[-1].start()
+    for load, store in zip(loads, stores):
+        load.wait()
+        store.start()
+    for store in stores:
+        store.wait()
+
+
+def move(image):
+    return pl.pallas_call(
+        move_kernel,
+        out_shape=jax.ShapeDtypeStruct(image.shape, image.dtype),
+        in_specs=[ANY],
+        out_specs=ANY,
+        scratch_shapes=[
+            pltpu.VMEM(image.shape, image.dtype),
+            pltpu.SemaphoreType.DMA((8,)),
+            pltpu.SemaphoreType.DMA((8,)),
+        ],
+        name="move",
+    )(image)
 
 
 def rank_in(groups, positions):
@@ -565,7 +631,7 @@
         earlier.reshape(2 * X, block_len),
         rng_size,
     )
-    return image.reshape(earlier.shape)
+    return move(image).reshape(earlier.shape)
 
 
 def solution(mesh):

time: 206 us -> 194 us (0.942)
  local copies, waits for them, and re-layouts: 11 us -> 2.54 us
  Pallas kernels: 188 us -> 185 us
    pallas_call x1, Pallas kernels: 188 us -> 178 us  [focus(): pl.pallas_call(functools.partial(image_kernel, rng_size), out_shape=jax.S...]
    unnamed x1 -> x0, local copies, waits for them, and re-layouts: 8.44 us -> none
    pallas_call x0 -> x1, Pallas kernels: none -> 6.42 us  [move(): pl.pallas_call(move_kernel, out_shape=jax.ShapeDtypeStruct(image.shape, i...]
where the time goes in v6:
time: 194 us; the launch traced here: 193 us
  Pallas kernels  185 us (95%)
  other arithmetic  5.32 us (3%)
  local copies, waits for them, and re-layouts  2.54 us (1%)
    pallas_call x1, Pallas kernels, focus(): pl.pallas_call(functools.partial(image_kernel, rng_size), out_shape=jax.S...  178 us
    pallas_call x1, Pallas kernels, move(): pl.pallas_call(move_kernel, out_shape=jax.ShapeDtypeStruct(image.shape, i...  6.42 us

profile of v6, /device:TPU:0, one launch (start us, length us, event | category | flops | bytes accessed | tf_op | source)
XLA Modules:
  0.0 192.9 jit_solution(12635282303213212020)
XLA Ops:
  0.0 0.1 pad_add_fusion.3
  0.1 0.8 select_reduce_fusion.2
  1.0 0.1 pad_add_fusion.4
  1.2 0.1 fusion.10
  1.2 0.9 multiply_reduce_fusion.1
  2.2 0.1 fusion.9
  2.3 0.1 broadcast_compare_fusion
  2.4 0.5 convert_reduce_fusion
  2.9 0.6 select_reduce_fusion.1
  3.5 0.1 stack_reshape.6
  3.6 0.1 stack_reshape.7
  3.7 0.6 pad_add_fusion.1.table
  4.3 0.1 add_add_fusion
  4.4 0.1 slice_reduce_fusion
  4.5 0.6 select_add_fusion.arrival
  5.1 0.7 slice_bitcast_fusion
  5.8 0.1 copy.31
  5.9 0.1 copy.30
  6.0 0.7 copy.32.list_ref
  6.7 0.7 copy.33.scale_ref
  7.3 0.7 fusion.1
  8.1 178.2 %focus.1.source = bf16[2048,2048]{1,0:T(8,128)(2,1)} custom-call(s32[2,128]{1,0:T(2,128)} %pad_add_fusion.1.table, s32[2,48]{1,0:T(2,128)} %select_add_fusion.arrival, bf16[16,2,32,2048]{3,2,1,0:T(8,128)(2,1)} %echo_ref.1, bf16[16,8,32]{2,1,0:T(8,128)(2,1)} %get-tuple-element.23.front_ref, bf16[16,8,32]{2,1,0:T(8,128)(2,1)} %get-tuple-element.24.rear_ref, ...), custom_call_target="tpu_custom_call" | custom-call | tf_op jit(solution)/shard_map/focus/pallas_call | solution.py:493
  186.3 6.4 %move.1 = bf16[2048,2048]{1,0:T(8,128)(2,1)} custom-call(bf16[2048,2048]{1,0:T(8,128)(2,1)} %focus.1.source), custom_call_target="tpu_custom_call" | custom-call | tf_op jit(solution)/shard_map/move/pallas_call | solution.py:546
  (14 shorter events, 0.1 us)

commit v7 on v6

--- a/solution.py
+++ b/solution.py
@@ -18,7 +18,6 @@
 HOLD = 8
 MESH = pl.DeviceIdType.MESH
 ANY = pl.BlockSpec(memory_space=pl.ANY)
-IN_VMEM = pl.BlockSpec(memory_space=pltpu.VMEM)
 
 phase_modulus = 4099
 small_value = 1e-06
@@ -65,15 +64,15 @@
 
 def image_kernel(
     rng_size,
+    footprint,
+    counts,
+    offsets,
+    pairing,
+    echo_ref,
+    earlier_ref,
+    out_ref,
     table,
     arrival,
-    echo_ref,
-    front_ref,
-    rear_ref,
-    list_ref,
-    scale_ref,
-    earlier_ref,
-    out_ref,
     row_first,
     row_second,
     column_first,
@@ -236,6 +235,59 @@
     use_low = level > 0
     use_high = level < rng_size - 1
 
+    def owner_of(ping):
+        owner = ping >> 4
+        return owner >> 3, (owner >> 1) & (SIDE - 1), owner & (CORES - 1)
+
+    for part in range(2):
+        for k in range(HOLD):
+            d, dc = k // CORES, k % CORES
+            tile_id = device(y + d, x, c + dc) if part == 0 else device(y, x + d, c + dc)
+            limit = counts[tile_id]
+
+            def scan(j, carry, part=part, tile_id=tile_id, limit=limit):
+                filled, sources, shifts = carry
+                ping = footprint[tile_id, j]
+                oy, ox, oc = owner_of(ping)
+                near = oy == y if part == 0 else ox == x
+                match = near & (oc == c) & (j < limit)
+                away = (ox - x if part == 0 else oy - y) + SIDE
+                source = (away & (SIDE - 1)) * PING_DEV + (ping & (PING_DEV - 1))
+                shift = offsets[tile_id, j]
+                at = jnp.where(match, filled, -1)
+                sources = tuple(jnp.where(at == i, source, v) for i, v in enumerate(sources))
+                shifts = tuple(jnp.where(at == i, shift, v) for i, v in enumerate(shifts))
+                return filled + match.astype(jnp.int32), sources, shifts
+
+            zeros = (jnp.int32(0),) * HOLD
+            _, sources, shifts = lax.fori_loop(0, MOST, scan, (jnp.int32(0), zeros, zeros))
+            for i in range(HOLD):
+                table[0, (part * HOLD + k) * HOLD + i] = sources[i]
+                table[1, (part * HOLD + k) * HOLD + i] = shifts[i]
+
+    own_limit = counts[me]
+    for part in range(2):
+
+        def scan_own(j, carry, part=part):
+            first, held = carry
+            oy, ox, oc = owner_of(footprint[me, j])
+            at = oy if part == 0 else ox
+            group = at * CORES + oc
+            rank = jnp.int32(0)
+            for g in range(HOLD):
+                rank = jnp.where(group == g, held[g], rank)
+            away = ((y if part == 0 else x) - at + SIDE) & (SIDE - 1)
+            core = (c - oc + CORES) & (CORES - 1)
+            slot = ((part * SIDE + away) * CORES + core) * HOLD + rank
+            first = jnp.where(j == 0, slot, first)
+            listed = j < own_limit
+            arrival[part, j] = jnp.where(listed, slot, first)
+            entered = jnp.where(listed, group, -1)
+            held = tuple(v + jnp.where(entered == g, 1, 0) for g, v in enumerate(held))
+            return first, held
+
+        lax.fori_loop(0, MOST, scan_own, (jnp.int32(0), (jnp.int32(0),) * HOLD))
+
     for copy in own:
         copy.wait()
     from_lead.wait_recv()
@@ -248,8 +300,17 @@
         out = jnp.sum(out, axis=0, keepdims=True)
         return jnp.sum(out, axis=1, keepdims=True)
 
+    pair_row = lax.broadcasted_iota(jnp.int32, (8, C), 0)
+    channel = lax.broadcasted_iota(jnp.int32, (8, C), 1)
+
+    def picks(p, side):
+        wanted = jnp.zeros((8, C), jnp.int32)
+        for k in range(8):
+            wanted = jnp.where(pair_row == k, pairing[p, side, k], wanted)
+        return jnp.where(channel == wanted, 1.0, 0.0).astype(jnp.bfloat16)
+
     def correlate(p, front_source, acc):
-        front, rear = front_ref[p], rear_ref[p]
+        front, rear = picks(p, 0), picks(p, 1)
         dot = functools.partial(jnp.dot, preferred_element_type=jnp.float32)
         cross = front_energy = rear_energy = 0.0
         for h in range(2):
@@ -319,21 +380,35 @@
         copy.wait_recv()
 
     chirp = cosines.shape[1]
+    entry = lax.broadcasted_iota(jnp.int32, (MOST, 128), 0)
+    foot = jnp.zeros((MOST, 128), jnp.int32)
+    shift = jnp.zeros((MOST, 128), jnp.int32)
+    for j in range(MOST):
+        foot = jnp.where(entry == j, footprint[me, j], foot)
+        shift = jnp.where(entry == j, offsets[me, j], shift)
+    listed = jnp.where(entry < own_limit, 1.0, 0.0)
+    channels = jnp.full((MOST, 128), own_limit, jnp.int32).astype(jnp.float32) * jnp.float32(C)
+    scale = (listed / jnp.sqrt(channels))[:, 0:1]
+
+    def modulo(value):
+        value = value - phase_modulus * (
+            value.astype(jnp.float32) * (1.0 / phase_modulus)
+        ).astype(jnp.int32)
+        value = jnp.where(value < 0, value + phase_modulus, value)
+        return jnp.where(value >= phase_modulus, value - phase_modulus, value)
+
+    lift = (owners * X // phase_modulus + 1) * phase_modulus
+    start = modulo(lift + me * X - foot * SPACING - 2 * (C - 1))
     along = lax.broadcasted_iota(jnp.int32, (MOST, chirp), 1)
-    turn = turns_of(sums, list_ref[:, 0:1], list_ref[:, 1:2])
-    folded = list_ref[:, 2:3] + along
+    turn = turns_of(sums, foot >> 4, foot & (PING_DEV - 1))
+    folded = start[:, 0:1] + along
     folded = jnp.where(folded >= phase_modulus, folded - phase_modulus, folded)
-    square = folded * folded
-    square = square - phase_modulus * (
-        square.astype(jnp.float32) * (1.0 / phase_modulus)
-    ).astype(jnp.int32)
-    square = jnp.where(square < 0, square + phase_modulus, square)
-    square = jnp.where(square >= phase_modulus, square - phase_modulus, square)
+    square = modulo(folded * folded)
     phases = square.astype(jnp.float32) * (2.0 * math.pi / phase_modulus) + (
-        list_ref[:, 3:4].astype(jnp.float32) * (math.pi / 4.0) - turn
+        shift[:, 0:1].astype(jnp.float32) * (math.pi / 4.0) - turn
     )
-    cosines[...] = jnp.cos(phases) * scale_ref[:, 0:1]
-    sines[...] = jnp.sin(phases) * scale_ref[:, 0:1]
+    cosines[...] = jnp.cos(phases) * scale
+    sines[...] = jnp.sin(phases) * scale
 
     def spread(ref, j):
         return pltpu.roll(
@@ -479,7 +554,7 @@
         copy.wait()
 
 
-def focus(table, arrival, echoes, front_pick, rear_pick, entries, scales, earlier, rng_size):
+def focus(footprint, counts, offsets, pairing, echoes, earlier, rng_size):
     pings, parts, channels, length = echoes.shape
     owners = SIDE * SIDE * CORES
     chunks = 8
@@ -493,9 +568,11 @@
     return pl.pallas_call(
         functools.partial(image_kernel, rng_size),
         out_shape=jax.ShapeDtypeStruct((2 * X, length), bf16),
-        in_specs=[smem, smem, ANY, IN_VMEM, IN_VMEM, IN_VMEM, IN_VMEM, ANY],
+        in_specs=[smem] * 4 + [ANY, ANY],
         out_specs=ANY,
         scratch_shapes=[
+            pltpu.SMEM((2, slots), jnp.int32),
+            pltpu.SMEM((2, MOST), jnp.int32),
             *[pltpu.VMEM((SIDE * pings, channels, length // 2), bf16)] * 4,
             *[pltpu.VMEM((SIDE * pings, channels, 128), bf16)] * 4,
             pltpu.VMEM((parts, channels, length), bf16),
@@ -523,7 +600,7 @@
             collective_id=0, has_side_effects=True, vmem_limit_bytes=63 << 20
         ),
         name="focus",
-    )(table, arrival, echoes, front_pick, rear_pick, entries, scales, earlier)
+    )(footprint, counts, offsets, pairing, echoes, earlier)
 
 
 def move_kernel(source, target, held, load_sem, store_sem):
@@ -557,78 +634,15 @@
     )(image)
 
 
-def rank_in(groups, positions):
-    same = (groups[:, None, :] == groups[:, :, None]) & (positions[None, :] < positions[:, None])[None]
-    return jnp.sum(same.astype(jnp.int32), axis=2)
-
-
 def per_device(echoes, pairing, footprint, counts, offsets, earlier):
-    block_len = echoes.shape[3]
-    owners = lax.axis_size("ping")
     rng_size = lax.axis_size("rng")
-    me = lax.axis_index("ping")
-    y, x, c = place(me)
-
-    channel_ids = jnp.arange(C, dtype=jnp.int32)
-    front_pick = (pairing[:, 0, :, None] == channel_ids).astype(jnp.bfloat16)
-    rear_pick = (pairing[:, 1, :, None] == channel_ids).astype(jnp.bfloat16)
-
-    steps = jnp.arange(HOLD, dtype=jnp.int32)
-    tiles = jnp.concatenate(
-        [
-            device(y + steps // CORES, x, c + steps % CORES),
-            device(y, x + steps // CORES, c + steps % CORES),
-        ]
-    )
-    all_tiles = jnp.arange(owners, dtype=jnp.int32)
-    chosen = (tiles[:, None] == all_tiles[None, :]).astype(jnp.int32)
-    positions = jnp.arange(MOST, dtype=jnp.int32)
-    foot = jnp.sum(chosen[:, :, None] * footprint[None], axis=1)
-    shift = jnp.sum(chosen[:, :, None] * offsets[None], axis=1)
-    count = jnp.sum(chosen * counts[None, :], axis=1)
-    listed = positions[None, :] < count[:, None]
-    oy, ox, oc = place(foot // PING_DEV)
-    by_row = steps[:, None] >= 0
-    by_row = jnp.concatenate([by_row, ~by_row], axis=0)
-    group = jnp.where(listed, jnp.where(by_row, oy, ox) * CORES + oc, -1)
-    rank = rank_in(group, positions)
-    here = group == jnp.where(by_row, y, x) * CORES + c
-    distance = jnp.where(by_row, ox - x + SIDE, oy - y + SIDE) % SIDE
-    source = distance * PING_DEV + foot % PING_DEV
-    fits = (here[:, None, :] & (rank[:, None, :] == steps[None, :, None])).astype(jnp.int32)
-    table = jnp.stack(
-        [
-            jnp.sum(fits * source[:, None, :], axis=2).reshape(-1),
-            jnp.sum(fits * shift[:, None, :], axis=2).reshape(-1),
-        ]
-    )
-    own_group = jnp.stack([group[0], group[HOLD]])
-    own_rank = jnp.stack([rank[0], rank[HOLD]])
-    own_place = jnp.stack([y, x])[:, None]
-    own_distance = (own_place - own_group // CORES + SIDE) % SIDE
-    own_core = (c - own_group % CORES + CORES) % CORES
-    arrival = (own_distance * CORES + own_core) * HOLD + own_rank
-    arrival = jnp.where(listed[0:1], arrival, arrival[:, 0:1])
-    arrival = arrival + jnp.array([[0], [HOLD * HOLD]], jnp.int32)
-    entries = jnp.stack(
-        [
-            foot[0] // PING_DEV,
-            foot[0] % PING_DEV,
-            jnp.remainder(me * X - foot[0] * SPACING - 2 * (C - 1), phase_modulus),
-            shift[0],
-        ],
-        axis=1,
-    )
-    scales = listed[0].astype(jnp.float32) / jnp.sqrt(jnp.float32(C) * count[0].astype(jnp.float32))
     image = focus(
-        table,
-        arrival,
+        footprint,
+        counts,
+        offsets,
+        pairing,
         echoes,
-        front_pick,
-        rear_pick,
-        entries,
-        scales[:, None],
-        earlier.reshape(2 * X, block_len),
+        earlier.reshape(2 * X, echoes.shape[3]),
         rng_size,
     )
     return move(image).reshape(earlier.shape)

time: 194 us -> 188 us (0.969)
  other arithmetic: 5.32 us -> 0 us
    reduce_sum x4 -> x0, other arithmetic: 2.84 us -> none  [the longest x1 0.9 us: per_device(): foot = jnp.sum(chosen[:, :, None] * footprint[None], axis=1)]
where the time goes in v7:
time: 188 us; the launch traced here: 187 us
  Pallas kernels  185 us (98%)
    pallas_call x1, Pallas kernels, focus(): pl.pallas_call(functools.partial(image_kernel, rng_size), out_shape=jax.S...  179 us
    pallas_call x1, Pallas kernels, move(): pl.pallas_call(move_kernel, out_shape=jax.ShapeDtypeStruct(image.shape, i...  6.42 us

profile of v7, /device:TPU:0, one launch (start us, length us, event | category | flops | bytes accessed | tf_op | source)
XLA Modules:
  0.0 186.8 jit_solution(5052865625688247299)
XLA Ops:
  0.0 1.4 copy.7.pairing
  1.4 178.9 %focus.1.source = bf16[2048,2048]{1,0:T(8,128)(2,1)} custom-call(s32[32,48]{1,0:T(8,128)} %footprint.1, s32[32]{0:T(128)} %counts.1, s32[32,48]{1,0:T(8,128)} %offsets.1, s32[16,2,8]{2,1,0:T(2,128)} %copy.7.pairing, bf16[16,2,32,2048]{3,2,1,0:T(8,128)(2,1)} %echo_ref.1, bf16[2048,2048]{1,0:T(8,128)(2,1)} %bitcast.2), custom_call_target="tpu_custom_call" | custom-call | tf_op jit(solution)/shard_map/focus/pallas_call | solution.py:568
  180.3 6.4 %move.1 = bf16[2048,2048]{1,0:T(8,128)(2,1)} custom-call(bf16[2048,2048]{1,0:T(8,128)(2,1)} %focus.1.source), custom_call_target="tpu_custom_call" | custom-call | tf_op jit(solution)/shard_map/move/pallas_call | solution.py:623

commit v8 on v7

--- a/solution.py
+++ b/solution.py
@@ -170,11 +170,6 @@
     behind = {"ping": device(y, x - 1, c)}
     above = {"ping": device(y + 1, x, c)}
     below = {"ping": device(y - 1, x, c)}
-    low, high = pl.ds(0, half), pl.ds(half, half)
-
-    def part_of(distance, start):
-        return pl.ds(distance * pings + start, half)
-
     from_lead = send(echo_ref.at[pings - 1], lead, {"ping": (me + 1) % owners})
 
     edge_copies = []
@@ -212,21 +207,28 @@
         pl.ds(0, pings),
     )
     ways = ((0, ahead, behind), (1, above, below))
+    pieces = [
+        [((0, m), (m, pings - m)) for m in ((half - 1, half) if part == 0 else (half, half))]
+        for part in range(2)
+    ]
     forward, backward = [[], []], [[], []]
     for h in range(2):
         for turn in range(2):
             for part, forth, back in ways:
-                first, second = (low, high) if turn == 0 else (high, low)
                 pool = pools[part][h]
+                at, size = pieces[part][h][turn]
                 forward[h].append(
                     send(
-                        echo_ref.at[first, part, :, spans[h]], pool.at[part_of(3, turn * half)], forth
+                        echo_ref.at[pl.ds(at, size), part, :, spans[h]],
+                        pool.at[pl.ds(3 * pings + at, size)],
+                        forth,
                     )
                 )
+                at, size = pieces[part][h][1 - turn]
                 backward[h].append(
                     send(
-                        echo_ref.at[second, part, :, spans[h]],
-                        pool.at[part_of(1, (1 - turn) * half)],
+                        echo_ref.at[pl.ds(at, size), part, :, spans[h]],
+                        pool.at[pl.ds(pings + at, size)],
                         back,
                     )
                 )
@@ -372,10 +374,13 @@
     for h in range(2):
         for part, forth, back in ways:
             pool = pools[part][h]
+            (at, size), (later, rest) = pieces[part][h]
             forward[h][part].wait_recv()
-            relays[h].append(send(pool.at[part_of(3, 0)], pool.at[part_of(2, 0)], forth))
+            source, target = pl.ds(3 * pings + at, size), pl.ds(2 * pings + at, size)
+            relays[h].append(send(pool.at[source], pool.at[target], forth))
             backward[h][part].wait_recv()
-            relays[h].append(send(pool.at[part_of(1, half)], pool.at[part_of(2, half)], back))
+            source, target = pl.ds(pings + later, rest), pl.ds(2 * pings + later, rest)
+            relays[h].append(send(pool.at[source], pool.at[target], back))
     for copy in spread_sums:
         copy.wait_recv()
 

time: 188 us -> 188 us (level)
  no operation moved by 1% of the time
where the time goes in v8:
time: 188 us; the launch traced here: 186 us
  Pallas kernels  184 us (98%)
    pallas_call x1, Pallas kernels, focus(): pl.pallas_call(functools.partial(image_kernel, rng_size), out_shape=jax.S...  178 us
    pallas_call x1, Pallas kernels, move(): pl.pallas_call(move_kernel, out_shape=jax.ShapeDtypeStruct(image.shape, i...  6.42 us

profile of v8, /device:TPU:0, one launch (start us, length us, event | category | flops | bytes accessed | tf_op | source)
XLA Modules:
  0.0 186.0 jit_solution(11450282395899671852)
XLA Ops:
  0.0 1.4 copy.7.pairing
  1.4 178.1 %focus.1.source = bf16[2048,2048]{1,0:T(8,128)(2,1)} custom-call(s32[32,48]{1,0:T(8,128)} %footprint.1, s32[32]{0:T(128)} %counts.1, s32[32,48]{1,0:T(8,128)} %offsets.1, s32[16,2,8]{2,1,0:T(2,128)} %copy.7.pairing, bf16[16,2,32,2048]{3,2,1,0:T(8,128)(2,1)} %echo_ref.1, bf16[2048,2048]{1,0:T(8,128)(2,1)} %bitcast.2), custom_call_target="tpu_custom_call" | custom-call | tf_op jit(solution)/shard_map/focus/pallas_call | solution.py:573
  179.4 6.4 %move.1 = bf16[2048,2048]{1,0:T(8,128)(2,1)} custom-call(bf16[2048,2048]{1,0:T(8,128)(2,1)} %focus.1.source), custom_call_target="tpu_custom_call" | custom-call | tf_op jit(solution)/shard_map/move/pallas_call | solution.py:628
